TPU v7x, 128 devices: a whole 4x4x4 slice. The times are simulated.
128 devices in a mesh: seq: 16 (over x, y), enc: 8 (over z, core).
Axes of the slice: x: 4, y: 4, z: 4, core: 2. Of those that a mesh axis runs over, the one named last changes fastest.
Arguments:
- queries: bfloat16 [2048, 8192], P('seq', 'enc'), may hold values from -63 to 63
- image_key_value: bfloat16 [2, 128, 1601, 1024], P(None, ('seq', 'enc')), may hold values from -16 to 16
- image_spans: int32 [32, 2], replicated, may hold values from 0 to 2048, as said below
- tile_counts: int32 [32], replicated, may hold values from 1 to 4
- cross_gate: float32 [1], replicated, may hold values from 0.2 to 2
- grad_out: bfloat16 [2048, 8192], P('seq', 'enc'), may hold values from -6 to 6
Outputs:
- attended: bfloat16 [2048, 8192], P('seq', 'enc')
- grad_queries: bfloat16 [2048, 8192], P('seq', 'enc')
- grad_image_kv: bfloat16 [2, 128, 1601, 1024], P(None, ('seq', 'enc'))
Inputs may be any that keep to these rules, and one draw needn't show every extreme that they name: `image_spans`: image m owns tiles 4 m to 4 m + 3. Its span starts in text shard m // 2 (positions (m // 2) * 128 to (m // 2) * 128 + 127), starts do not fall from one image to the next within a shard, and each span holds 1 to 128 positions.
All inputs are finite; a program needn't handle non-finite values.
Results may differ from a plain program's by a relative error of at most 0.0062.
Values may be sent and summed in bfloat16 or wider, within the bound.
A program may use at most 128 MiB of HBM per device.

v0:
```python
import jax
import jax.numpy as jnp
from jax import lax
from jax.sharding import PartitionSpec as P

HEAD_SIZE = 128
TILES = 4


NEG_FILL = -1e30


def shifted(shard, axis, by):
    devices = lax.axis_size(axis)
    pairs = [(i, i + by) for i in range(devices) if 0 <= i + by < devices]
    return lax.ppermute(shard, axis, pairs)


def visible_rows(image_spans, tile_counts, first_tile, tile_total, first_text, text_rows):
    image_total = image_spans.shape[0]
    tile_ids = first_tile + jnp.arange(tile_total, dtype=jnp.int32)
    image_ids = jnp.floor_divide(tile_ids, TILES)
    slot_ids = tile_ids - image_ids * TILES
    lookup = (image_ids[:, None] == jnp.arange(image_total, dtype=jnp.int32)[None, :]).astype(
        jnp.int32
    )
    starts = jnp.sum(lookup * image_spans[:, 0][None, :], axis=1)
    span_ends = jnp.sum(lookup * image_spans[:, 1][None, :], axis=1)
    in_use = jnp.sum(lookup * tile_counts[None, :], axis=1)
    usable = (tile_ids >= 0) & (slot_ids < in_use)
    positions = first_text + jnp.arange(text_rows, dtype=jnp.int32)
    return (
        usable[None, :]
        & (positions[:, None] >= starts[None, :])
        & (positions[:, None] < span_ends[None, :])
    )


def keep_state(stats_now):
    return stats_now


def score_block(query_head, key_tile, softmax_scale):
    return (
        jnp.einsum("tgd,jd->tgj", query_head, key_tile, preferred_element_type=jnp.float32)
        * softmax_scale
    )


def forward_tiles(query_heads, key_tiles, value_tiles, visible, softmax_scale):
    active = jnp.any(visible, axis=0)
    columns = visible.T
    text_rows, local_heads, head_groups, head_dim = query_heads.shape
    query_head = query_heads[:, 0]
    head_keys = key_tiles[:, :, 0]
    head_values = value_tiles[:, :, 0]

    def online_step(carried, tile_item):
        key_tile, value_tile, column, tile_live = tile_item

        def online_update(state):
            run_max, run_total, run_out = state
            scores = score_block(query_head, key_tile, softmax_scale)
            row_mask = column[:, None, None]
            tile_max = jnp.max(jnp.where(row_mask, scores, NEG_FILL), axis=2)
            new_max = jnp.maximum(run_max, tile_max)
            factor = jnp.exp(run_max - new_max)
            probs = jnp.where(row_mask, jnp.exp(scores - new_max[:, :, None]), 0.0)
            new_total = run_total * factor + jnp.sum(probs, axis=2)
            new_out = run_out * factor[:, :, None] + jnp.einsum(
                "tgj,jd->tgd",
                probs.astype(jnp.bfloat16),
                value_tile,
                preferred_element_type=jnp.float32,
            )
            return (new_max, new_total, new_out)

        return (lax.cond(tile_live, online_update, keep_state, carried), None)

    starting_state = (
        jnp.full((text_rows, head_groups), NEG_FILL, jnp.float32),
        jnp.zeros((text_rows, head_groups), jnp.float32),
        jnp.zeros((text_rows, head_groups, head_dim), jnp.float32),
    )
    (run_max, run_total, run_out), unused = lax.scan(
        online_step, starting_state, (head_keys, head_values, columns, active)
    )
    seen = run_total > 0.0
    safe_total = jnp.where(seen, run_total, 1.0)
    log_total = jnp.where(seen, run_max + jnp.log(safe_total), 0.0)
    mixed_head = jnp.where(seen[:, :, None], run_out / safe_total[:, :, None], 0.0)
    outputs = [mixed_head]
    log_sums = [log_total]
    return (jnp.stack(outputs, 1), jnp.stack(log_sums, 1))


def backward_tiles(
    query_heads, grad_heads, log_totals, row_deltas, key_tiles, value_tiles, visible, softmax_scale
):
    active = jnp.any(visible, axis=0)
    columns = visible.T
    text_rows, local_heads, head_groups, head_dim = query_heads.shape
    query_head = query_heads[:, 0]
    grad_head = grad_heads[:, 0]
    log_total = log_totals[:, 0]
    row_delta = row_deltas[:, 0]
    head_keys = key_tiles[:, :, 0]
    head_values = value_tiles[:, :, 0]

    def grad_step(carried, tile_item):
        key_tile, value_tile, column, tile_live = tile_item

        def grad_update(running):
            scores = score_block(query_head, key_tile, softmax_scale)
            weights = jnp.where(column[:, None, None], jnp.exp(scores - log_total[:, :, None]), 0.0)
            weights_low = weights.astype(jnp.bfloat16)
            grad_weights = jnp.einsum(
                "tgd,jd->tgj", grad_head, value_tile, preferred_element_type=jnp.float32
            )
            grad_scores = (weights * (grad_weights - row_delta[:, :, None])).astype(jnp.bfloat16)
            new_running = (
                running
                + jnp.einsum(
                    "tgj,jd->tgd", grad_scores, key_tile, preferred_element_type=jnp.float32
                )
                * softmax_scale
            )
            key_term = (
                jnp.einsum(
                    "tgj,tgd->jd", grad_scores, query_head, preferred_element_type=jnp.float32
                )
                * softmax_scale
            ).astype(jnp.bfloat16)
            value_term = jnp.einsum(
                "tgj,tgd->jd", weights_low, grad_head, preferred_element_type=jnp.float32
            ).astype(jnp.bfloat16)
            return (new_running, (key_term, value_term))

        def passed(running):
            zero_rows = jnp.zeros(key_tile.shape, jnp.bfloat16)
            return (running, (zero_rows, zero_rows))

        return lax.cond(tile_live, grad_update, passed, carried)

    query_grad, (key_term, value_term) = lax.scan(
        grad_step,
        jnp.zeros((text_rows, head_groups, head_dim), jnp.float32),
        (head_keys, head_values, columns, active),
    )
    query_grads = [query_grad]
    key_grads = [key_term]
    value_grads = [value_term]
    return (jnp.stack(query_grads, 1), jnp.stack(key_grads, 2), jnp.stack(value_grads, 2))


def shards(queries, image_key_value, image_spans, tile_counts, cross_gate, grad_out):
    seq_index = lax.axis_index("seq")
    enc_total = lax.axis_size("enc")
    text_rows = queries.shape[0]
    tile_tokens = image_key_value.shape[2]
    local_heads = image_key_value.shape[3] // (enc_total * HEAD_SIZE)
    head_groups = queries.shape[1] // (local_heads * HEAD_SIZE)
    width = local_heads * HEAD_SIZE
    softmax_scale = HEAD_SIZE ** (-0.5)
    split_kv = image_key_value.reshape(2, 1, tile_tokens, enc_total, width)
    own_rows = lax.all_to_all(split_kv, "enc", split_axis=3, concat_axis=1, tiled=True)
    prev_rows = shifted(own_rows, "seq", 1)
    reach = jnp.concatenate([prev_rows, own_rows], 1)
    key_tiles = reach[0]
    value_tiles = reach[1]
    visible = visible_rows(
        image_spans,
        tile_counts,
        (seq_index - 1) * enc_total,
        2 * enc_total,
        seq_index * text_rows,
        text_rows,
    )
    query_heads = queries.reshape(text_rows, local_heads, head_groups, HEAD_SIZE)
    mixed, log_totals = forward_tiles(query_heads, key_tiles, value_tiles, visible, softmax_scale)
    gate_value = jnp.tanh(cross_gate[0])
    attended = (
        (gate_value * mixed)
        .reshape(text_rows, local_heads * head_groups * HEAD_SIZE)
        .astype(jnp.bfloat16)
    )
    gradient_blended = (gate_value * grad_out.astype(jnp.float32)).astype(jnp.bfloat16)
    grad_heads = gradient_blended.reshape(text_rows, local_heads, head_groups, HEAD_SIZE)
    row_deltas = jnp.sum(grad_heads.astype(jnp.float32) * mixed, axis=3)
    query_grad, key_term, value_term = backward_tiles(
        query_heads,
        grad_heads,
        log_totals,
        row_deltas,
        key_tiles,
        value_tiles,
        visible,
        softmax_scale,
    )
    terms = jnp.stack([key_term, value_term], 0)
    later_terms = shifted(terms[:, :enc_total], "seq", -1)
    row_grads = (terms[:, enc_total:].astype(jnp.float32) + later_terms.astype(jnp.float32)).astype(
        jnp.bfloat16
    )
    home_grads = lax.all_to_all(row_grads, "enc", split_axis=1, concat_axis=3, tiled=True)
    grad_image_kv = home_grads.reshape(2, 1, tile_tokens, enc_total * width)
    grad_queries = query_grad.reshape(text_rows, local_heads * head_groups * HEAD_SIZE).astype(
        jnp.bfloat16
    )
    return (attended, grad_queries, grad_image_kv)


def solution(mesh):
    in_specs = (
        P("seq", "enc"),
        P(None, ("seq", "enc"), None, None),
        P(),
        P(),
        P(),
        P("seq", "enc"),
    )
    out_specs = (P("seq", "enc"), P("seq", "enc"), P(None, ("seq", "enc"), None, None))
    return jax.shard_map(shards, mesh=mesh, in_specs=in_specs, out_specs=out_specs, check_vma=False)
```

profile of v0, /device:TPU:4, one launch (start us, length us, event | category | flops | bytes accessed | tf_op | source)
XLA Modules:
  0.0 863.5 jit_solution(7312457288802790035)
XLA Ops:
  6.6 81.2 %all_to_all.33 = bf16[2,1,1601,8,128]{4,0,2,1,3:T(2,128)(2,1)S(1)} all-to-all(bf16[2,1,1601,8,128]{4,0,2,1,3:T(2,128)(2,1)S(1)} %copy_bitcast_fusion), channel_id=1, replica_groups=mesh['seq'=16,'enc'=8] {'enc'}, dimensions={3} | all-to-all | bytes 13115392 | tf_op jit(solution)/shard_map/all_to_all | solution.py:166
  97.7 142.2 %collective-permute-done = bf16[2,8,1601,1,128]{4,1,3,2,0:T(8,128)(2,1)} collective-permute-done((bf16[2,8,1601,1,128]{4,1,3,2,0:T(8,128)(2,1)}, bf16[2,8,1601,1,128]{4,1,3,2,0:T(8,128)(2,1)}, u32[]{:S(2)}, u32[]{:S(2)}) %collective-permute-start) | collective-permute-done | bytes 6557728 | tf_op jit(solution)/shard_map/ppermute | solution.py:16
  255.0 134.5 %while.33 = (s32[]{:T(128)}, f32[128,8]{0,1:T(8,128)S(1)}, f32[128,8]{0,1:T(8,128)S(1)}, f32[128,8,128]{2,0,1:T(8,128)S(1)}, pred[16]{0:T(512)(128)(4,1)S(1)}, /...) while((s32[]{:T(128)}, f32[128,8]{0,1:T(8,128)S(1)}, ...), condition=%wide.region_9.10_spmd.clone, body=%wide.region_4.9_spmd.clone.sunk | while | flops 857683456 | bytes 21875008 | solution.py:85
  256.2 10.4 %conditional.6 = ((f32[128,8]{0,1:T(8,128)S(1)}, f32[128,8]{0,1:T(8,128)S(1)}, f32[128,8,128]{2,0,1:T(8,128)S(1)})) conditional(s32[]{:T(128)} %bitcast.140, (f32[128,8]{0,1:T(8,128)S(1)}, f32[128,8]{0,1:T(8,128)S(1)}, f32[128,8,128]{2,0,1:T(8,128)S(1)}) %tuple.109, (pred[16]{0:T(512)(128)(4,1)S(1)}, s32[]{:T(128)}, ...), branch_computations={%region_5.5_spmd, %region_6.8_spmd.clone} | conditional | flops 857683456 | bytes 21874760 | solution.py:78
  267.9 10.4 %conditional.6 = ((f32[128,8]{0,1:T(8,128)S(1)}, f32[128,8]{0,1:T(8,128)S(1)}, f32[128,8,128]{2,0,1:T(8,128)S(1)})) conditional(s32[]{:T(128)} %bitcast.140, (f32[128,8]{0,1:T(8,128)S(1)}, f32[128,8]{0,1:T(8,128)S(1)}, f32[128,8,128]{2,0,1:T(8,128)S(1)}) %tuple.109, (pred[16]{0:T(512)(128)(4,1)S(1)}, s32[]{:T(128)}, ...), branch_computations={%region_5.5_spmd, %region_6.8_spmd.clone} | conditional | flops 857683456 | bytes 21874760 | solution.py:78
  279.5 10.4 %conditional.6 = ((f32[128,8]{0,1:T(8,128)S(1)}, f32[128,8]{0,1:T(8,128)S(1)}, f32[128,8,128]{2,0,1:T(8,128)S(1)})) conditional(s32[]{:T(128)} %bitcast.140, (f32[128,8]{0,1:T(8,128)S(1)}, f32[128,8]{0,1:T(8,128)S(1)}, f32[128,8,128]{2,0,1:T(8,128)S(1)}) %tuple.109, (pred[16]{0:T(512)(128)(4,1)S(1)}, s32[]{:T(128)}, ...), branch_computations={%region_5.5_spmd, %region_6.8_spmd.clone} | conditional | flops 857683456 | bytes 21874760 | solution.py:78
  292.5 10.4 %conditional.6 = ((f32[128,8]{0,1:T(8,128)S(1)}, f32[128,8]{0,1:T(8,128)S(1)}, f32[128,8,128]{2,0,1:T(8,128)S(1)})) conditional(s32[]{:T(128)} %bitcast.140, (f32[128,8]{0,1:T(8,128)S(1)}, f32[128,8]{0,1:T(8,128)S(1)}, f32[128,8,128]{2,0,1:T(8,128)S(1)}) %tuple.109, (pred[16]{0:T(512)(128)(4,1)S(1)}, s32[]{:T(128)}, ...), branch_computations={%region_5.5_spmd, %region_6.8_spmd.clone} | conditional | flops 857683456 | bytes 21874760 | solution.py:78
  304.1 10.4 %conditional.6 = ((f32[128,8]{0,1:T(8,128)S(1)}, f32[128,8]{0,1:T(8,128)S(1)}, f32[128,8,128]{2,0,1:T(8,128)S(1)})) conditional(s32[]{:T(128)} %bitcast.140, (f32[128,8]{0,1:T(8,128)S(1)}, f32[128,8]{0,1:T(8,128)S(1)}, f32[128,8,128]{2,0,1:T(8,128)S(1)}) %tuple.109, (pred[16]{0:T(512)(128)(4,1)S(1)}, s32[]{:T(128)}, ...), branch_computations={%region_5.5_spmd, %region_6.8_spmd.clone} | conditional | flops 857683456 | bytes 21874760 | solution.py:78
  315.7 10.4 %conditional.6 = ((f32[128,8]{0,1:T(8,128)S(1)}, f32[128,8]{0,1:T(8,128)S(1)}, f32[128,8,128]{2,0,1:T(8,128)S(1)})) conditional(s32[]{:T(128)} %bitcast.140, (f32[128,8]{0,1:T(8,128)S(1)}, f32[128,8]{0,1:T(8,128)S(1)}, f32[128,8,128]{2,0,1:T(8,128)S(1)}) %tuple.109, (pred[16]{0:T(512)(128)(4,1)S(1)}, s32[]{:T(128)}, ...), branch_computations={%region_5.5_spmd, %region_6.8_spmd.clone} | conditional | flops 857683456 | bytes 21874760 | solution.py:78
  328.7 10.4 %conditional.6 = ((f32[128,8]{0,1:T(8,128)S(1)}, f32[128,8]{0,1:T(8,128)S(1)}, f32[128,8,128]{2,0,1:T(8,128)S(1)})) conditional(s32[]{:T(128)} %bitcast.140, (f32[128,8]{0,1:T(8,128)S(1)}, f32[128,8]{0,1:T(8,128)S(1)}, f32[128,8,128]{2,0,1:T(8,128)S(1)}) %tuple.109, (pred[16]{0:T(512)(128)(4,1)S(1)}, s32[]{:T(128)}, ...), branch_computations={%region_5.5_spmd, %region_6.8_spmd.clone} | conditional | flops 857683456 | bytes 21874760 | solution.py:78
  340.3 10.4 %conditional.6 = ((f32[128,8]{0,1:T(8,128)S(1)}, f32[128,8]{0,1:T(8,128)S(1)}, f32[128,8,128]{2,0,1:T(8,128)S(1)})) conditional(s32[]{:T(128)} %bitcast.140, (f32[128,8]{0,1:T(8,128)S(1)}, f32[128,8]{0,1:T(8,128)S(1)}, f32[128,8,128]{2,0,1:T(8,128)S(1)}) %tuple.109, (pred[16]{0:T(512)(128)(4,1)S(1)}, s32[]{:T(128)}, ...), branch_computations={%region_5.5_spmd, %region_6.8_spmd.clone} | conditional | flops 857683456 | bytes 21874760 | solution.py:78
  352.0 10.4 %conditional.6 = ((f32[128,8]{0,1:T(8,128)S(1)}, f32[128,8]{0,1:T(8,128)S(1)}, f32[128,8,128]{2,0,1:T(8,128)S(1)})) conditional(s32[]{:T(128)} %bitcast.140, (f32[128,8]{0,1:T(8,128)S(1)}, f32[128,8]{0,1:T(8,128)S(1)}, f32[128,8,128]{2,0,1:T(8,128)S(1)}) %tuple.109, (pred[16]{0:T(512)(128)(4,1)S(1)}, s32[]{:T(128)}, ...), branch_computations={%region_5.5_spmd, %region_6.8_spmd.clone} | conditional | flops 857683456 | bytes 21874760 | solution.py:78
  364.9 10.4 %conditional.6 = ((f32[128,8]{0,1:T(8,128)S(1)}, f32[128,8]{0,1:T(8,128)S(1)}, f32[128,8,128]{2,0,1:T(8,128)S(1)})) conditional(s32[]{:T(128)} %bitcast.140, (f32[128,8]{0,1:T(8,128)S(1)}, f32[128,8]{0,1:T(8,128)S(1)}, f32[128,8,128]{2,0,1:T(8,128)S(1)}) %tuple.109, (pred[16]{0:T(512)(128)(4,1)S(1)}, s32[]{:T(128)}, ...), branch_computations={%region_5.5_spmd, %region_6.8_spmd.clone} | conditional | flops 857683456 | bytes 21874760 | solution.py:78
  376.5 10.4 %conditional.6 = ((f32[128,8]{0,1:T(8,128)S(1)}, f32[128,8]{0,1:T(8,128)S(1)}, f32[128,8,128]{2,0,1:T(8,128)S(1)})) conditional(s32[]{:T(128)} %bitcast.140, (f32[128,8]{0,1:T(8,128)S(1)}, f32[128,8]{0,1:T(8,128)S(1)}, f32[128,8,128]{2,0,1:T(8,128)S(1)}) %tuple.109, (pred[16]{0:T(512)(128)(4,1)S(1)}, s32[]{:T(128)}, ...), branch_computations={%region_5.5_spmd, %region_6.8_spmd.clone} | conditional | flops 857683456 | bytes 21874760 | solution.py:78
  390.1 183.8 %while.34 = (s32[]{:T(128)}, f32[128,8,128]{2,0,1:T(8,128)S(1)}, bf16[16,1601,128]{2,1,0:T(8,128)(2,1)}, bf16[16,1601,128]{2,1,0:T(8,128)(2,1)}, pred[16]{0:T(51...) while((s32[]{:T(128)}, f32[128,8,128]{2,0,1:T(8,128)S(1)}, ...), condition=%wide.region_14.15_spmd.clone, body=%wide.region_11.14_spmd.clone.sunk | while | flops 2115734400 | bytes 35320000 | solution.py:145
  391.6 13.4 %conditional.7 = (f32[128,8,128]{2,0,1:T(8,128)S(1)}, bf16[1,1601,128]{2,1,0:T(8,128)(2,1)S(1)}, bf16[1,1601,128]{2,1,0:T(8,128)(2,1)S(1)}) conditional(s32[]{:T(128)} %bitcast.141, f32[128,8,128]{2,0,1:T(8,128)S(1)} %get-tuple-element.934, (pred[16]{0:T(512)(128)(4,1)S(1)}, s32[]{:T(128)}, bf16[16,1601,128]{2,1,0:T(8,128)(2,1)}, ...), branch_computations={%region_12.12_spmd, %region_13.13_spmd.clone} | conditional | flops 2115734400 | bytes 33676224 | solution.py:143
  407.2 13.4 %conditional.7 = (f32[128,8,128]{2,0,1:T(8,128)S(1)}, bf16[1,1601,128]{2,1,0:T(8,128)(2,1)S(1)}, bf16[1,1601,128]{2,1,0:T(8,128)(2,1)S(1)}) conditional(s32[]{:T(128)} %bitcast.141, f32[128,8,128]{2,0,1:T(8,128)S(1)} %get-tuple-element.934, (pred[16]{0:T(512)(128)(4,1)S(1)}, s32[]{:T(128)}, bf16[16,1601,128]{2,1,0:T(8,128)(2,1)}, ...), branch_computations={%region_12.12_spmd, %region_13.13_spmd.clone} | conditional | flops 2115734400 | bytes 33676224 | solution.py:143
  422.8 13.4 %conditional.7 = (f32[128,8,128]{2,0,1:T(8,128)S(1)}, bf16[1,1601,128]{2,1,0:T(8,128)(2,1)S(1)}, bf16[1,1601,128]{2,1,0:T(8,128)(2,1)S(1)}) conditional(s32[]{:T(128)} %bitcast.141, f32[128,8,128]{2,0,1:T(8,128)S(1)} %get-tuple-element.934, (pred[16]{0:T(512)(128)(4,1)S(1)}, s32[]{:T(128)}, bf16[16,1601,128]{2,1,0:T(8,128)(2,1)}, ...), branch_computations={%region_12.12_spmd, %region_13.13_spmd.clone} | conditional | flops 2115734400 | bytes 33676224 | solution.py:143
  440.7 13.4 %conditional.7 = (f32[128,8,128]{2,0,1:T(8,128)S(1)}, bf16[1,1601,128]{2,1,0:T(8,128)(2,1)S(1)}, bf16[1,1601,128]{2,1,0:T(8,128)(2,1)S(1)}) conditional(s32[]{:T(128)} %bitcast.141, f32[128,8,128]{2,0,1:T(8,128)S(1)} %get-tuple-element.934, (pred[16]{0:T(512)(128)(4,1)S(1)}, s32[]{:T(128)}, bf16[16,1601,128]{2,1,0:T(8,128)(2,1)}, ...), branch_computations={%region_12.12_spmd, %region_13.13_spmd.clone} | conditional | flops 2115734400 | bytes 33676224 | solution.py:143
  456.4 13.4 %conditional.7 = (f32[128,8,128]{2,0,1:T(8,128)S(1)}, bf16[1,1601,128]{2,1,0:T(8,128)(2,1)S(1)}, bf16[1,1601,128]{2,1,0:T(8,128)(2,1)S(1)}) conditional(s32[]{:T(128)} %bitcast.141, f32[128,8,128]{2,0,1:T(8,128)S(1)} %get-tuple-element.934, (pred[16]{0:T(512)(128)(4,1)S(1)}, s32[]{:T(128)}, bf16[16,1601,128]{2,1,0:T(8,128)(2,1)}, ...), branch_computations={%region_12.12_spmd, %region_13.13_spmd.clone} | conditional | flops 2115734400 | bytes 33676224 | solution.py:143
  472.0 13.4 %conditional.7 = (f32[128,8,128]{2,0,1:T(8,128)S(1)}, bf16[1,1601,128]{2,1,0:T(8,128)(2,1)S(1)}, bf16[1,1601,128]{2,1,0:T(8,128)(2,1)S(1)}) conditional(s32[]{:T(128)} %bitcast.141, f32[128,8,128]{2,0,1:T(8,128)S(1)} %get-tuple-element.934, (pred[16]{0:T(512)(128)(4,1)S(1)}, s32[]{:T(128)}, bf16[16,1601,128]{2,1,0:T(8,128)(2,1)}, ...), branch_computations={%region_12.12_spmd, %region_13.13_spmd.clone} | conditional | flops 2115734400 | bytes 33676224 | solution.py:143
  490.0 13.4 %conditional.7 = (f32[128,8,128]{2,0,1:T(8,128)S(1)}, bf16[1,1601,128]{2,1,0:T(8,128)(2,1)S(1)}, bf16[1,1601,128]{2,1,0:T(8,128)(2,1)S(1)}) conditional(s32[]{:T(128)} %bitcast.141, f32[128,8,128]{2,0,1:T(8,128)S(1)} %get-tuple-element.934, (pred[16]{0:T(512)(128)(4,1)S(1)}, s32[]{:T(128)}, bf16[16,1601,128]{2,1,0:T(8,128)(2,1)}, ...), branch_computations={%region_12.12_spmd, %region_13.13_spmd.clone} | conditional | flops 2115734400 | bytes 33676224 | solution.py:143
  505.6 13.4 %conditional.7 = (f32[128,8,128]{2,0,1:T(8,128)S(1)}, bf16[1,1601,128]{2,1,0:T(8,128)(2,1)S(1)}, bf16[1,1601,128]{2,1,0:T(8,128)(2,1)S(1)}) conditional(s32[]{:T(128)} %bitcast.141, f32[128,8,128]{2,0,1:T(8,128)S(1)} %get-tuple-element.934, (pred[16]{0:T(512)(128)(4,1)S(1)}, s32[]{:T(128)}, bf16[16,1601,128]{2,1,0:T(8,128)(2,1)}, ...), branch_computations={%region_12.12_spmd, %region_13.13_spmd.clone} | conditional | flops 2115734400 | bytes 33676224 | solution.py:143
  521.1 13.4 %conditional.7 = (f32[128,8,128]{2,0,1:T(8,128)S(1)}, bf16[1,1601,128]{2,1,0:T(8,128)(2,1)S(1)}, bf16[1,1601,128]{2,1,0:T(8,128)(2,1)S(1)}) conditional(s32[]{:T(128)} %bitcast.141, f32[128,8,128]{2,0,1:T(8,128)S(1)} %get-tuple-element.934, (pred[16]{0:T(512)(128)(4,1)S(1)}, s32[]{:T(128)}, bf16[16,1601,128]{2,1,0:T(8,128)(2,1)}, ...), branch_computations={%region_12.12_spmd, %region_13.13_spmd.clone} | conditional | flops 2115734400 | bytes 33676224 | solution.py:143
  539.1 13.4 %conditional.7 = (f32[128,8,128]{2,0,1:T(8,128)S(1)}, bf16[1,1601,128]{2,1,0:T(8,128)(2,1)S(1)}, bf16[1,1601,128]{2,1,0:T(8,128)(2,1)S(1)}) conditional(s32[]{:T(128)} %bitcast.141, f32[128,8,128]{2,0,1:T(8,128)S(1)} %get-tuple-element.934, (pred[16]{0:T(512)(128)(4,1)S(1)}, s32[]{:T(128)}, bf16[16,1601,128]{2,1,0:T(8,128)(2,1)}, ...), branch_computations={%region_12.12_spmd, %region_13.13_spmd.clone} | conditional | flops 2115734400 | bytes 33676224 | solution.py:143
  554.7 13.4 %conditional.7 = (f32[128,8,128]{2,0,1:T(8,128)S(1)}, bf16[1,1601,128]{2,1,0:T(8,128)(2,1)S(1)}, bf16[1,1601,128]{2,1,0:T(8,128)(2,1)S(1)}) conditional(s32[]{:T(128)} %bitcast.141, f32[128,8,128]{2,0,1:T(8,128)S(1)} %get-tuple-element.934, (pred[16]{0:T(512)(128)(4,1)S(1)}, s32[]{:T(128)}, bf16[16,1601,128]{2,1,0:T(8,128)(2,1)}, ...), branch_computations={%region_12.12_spmd, %region_13.13_spmd.clone} | conditional | flops 2115734400 | bytes 33676224 | solution.py:143
  573.9 23.9 %copy_bitcast_fusion.1 = (bf16[1,16,1601,1,128]{4,1,3,2,0:T(8,128)(2,1)S(1)}, bf16[1,16,1601,1,128]{4,1,3,2,0:T(8,128)(2,1)S(1)}) fusion(bf16[16,1601,128]{2,1,0:T(8,128)(2,1)} %get-tuple-element.289, bf16[16,1601,128]{2,1,0:T(8,128)(2,1)} %get-tuple-element.288), kind=kLoop, calls=%fused_computation.71 | loop fusion | bytes 26230784 | tf_op jit(solution)/shard_map/stack;stack | solution.py:200
  600.3 142.3 %collective-permute-done.1 = bf16[2,8,1601,1,128]{4,1,3,2,0:T(8,128)(2,1)S(1)} collective-permute-done((bf16[2,8,1601,1,128]{4,1,3,2,0:T(8,128)(2,1)S(1)}, bf16[2,8,1601,1,128]{4,1,3,2,0:T(8,128)(2,1)S(1)}, u32[]{:S(2)}, u32[]{:S(2)}) %collective-permute-start.1) | collective-permute-done | bytes 6557728 | tf_op jit(solution)/shard_map/ppermute | solution.py:16
  744.3 18.0 %copy.119 = bf16[2,8,1601,1,128]{4,0,3,2,1:T(2,128)(2,1)} copy(bf16[2,8,1601,1,128]{4,1,3,2,0:T(8,128)(2,1)S(1)} %add_convert_fusion) | data formatting | bytes 13115392 | tf_op jit(solution)/shard_map/convert_element_type | solution.py:202
  768.7 73.4 %all-to-all-done.1 = bf16[2,8,1601,1,128]{4,0,3,2,1:T(2,128)(2,1)} async-done(((bf16[2,8,1601,1,128]{4,0,3,2,1:T(2,128)(2,1)}), bf16[2,8,1601,1,128]{4,0,3,2,1:T(2,128)(2,1)}, u32[]{:S(2)}, u32[]{:S(2)}) %all-to-all-start.1) | async-done | bytes 6557728 | tf_op jit(solution)/shard_map/all_to_all | solution.py:205
  842.1 8.2 copy.125
  850.3 13.3 %reshape.103 = bf16[2,1,1601,1024]{3,0,2,1:T(2,128)(2,1)} reshape(bf16[2,1,1601,8,1,128]{5,3,0,2,4,1:T(8,128)(2,1)} %copy.125) | data formatting | bytes 13115392
  (317 shorter events, 337.2 us)
Async XLA Ops:
  87.8 8.2 copy-start
  87.8 8.6 copy-start.1
  87.8 9.5 %copy-start.2 = (s32[32,2]{0,1:T(2,128)S(1)}, s32[32,2]{0,1:T(2,128)}, u32[]{:S(2)}) copy-start(s32[32,2]{0,1:T(2,128)} %param.16) | copy-start | bytes 772
  87.8 9.5 %copy-start.3 = (s32[32]{0:T(128)S(1)}, s32[32]{0:T(128)}, u32[]{:S(2)}) copy-start(s32[32]{0:T(128)} %param.17) | copy-start | bytes 388
  92.5 147.5 %collective-permute-start = (bf16[2,8,1601,1,128]{4,1,3,2,0:T(8,128)(2,1)}, bf16[2,8,1601,1,128]{4,1,3,2,0:T(8,128)(2,1)}, u32[]{:S(2)}, u32[]{:S(2)}) collective-permute-start(bf16[2,8,1601,1,128]{4,1,3,2,0:T(8,128)(2,1)} %bitcast.137), channel_id=1, source_target_pairs={{0,8},{8,16},{16,24},{24,32},{32,40},{40,48},{48,56},{56,64},{64,7... | collective-permute-start | bytes 19673096 | tf_op jit(solution)/shard_map/ppermute | solution.py:16
  598.3 144.2 %collective-permute-start.1 = (bf16[2,8,1601,1,128]{4,1,3,2,0:T(8,128)(2,1)S(1)}, bf16[2,8,1601,1,128]{4,1,3,2,0:T(8,128)(2,1)S(1)}, u32[]{:S(2)}, u32[]{:S(2)}) collective-permute-start(bf16[2,8,1601,1,128]{4,1,3,2,0:T(8,128)(2,1)S(1)} %pad_maximum_fusion), channel_id=1, source_target_pairs={{8,0},{16,8},{24,16},{32,24},{40,32},{48,40},{56,48},{64,56},{72,6... | collective-permute-start | bytes 19673096 | tf_op jit(solution)/shard_map/ppermute | solution.py:16
  762.3 79.8 %all-to-all-start.1 = ((bf16[2,8,1601,1,128]{4,0,3,2,1:T(2,128)(2,1)}), bf16[2,8,1601,1,128]{4,0,3,2,1:T(2,128)(2,1)}, u32[]{:S(2)}, u32[]{:S(2)}) async-start(bf16[2,8,1601,1,128]{4,0,3,2,1:T(2,128)(2,1)} %copy.119), calls=%async_computation.1 | async-start | bytes 13115392 | tf_op jit(solution)/shard_map/all_to_all | solution.py:205
where the time goes:
time: 867 us; the launch traced here: 864 us
  waiting for transfers between devices  358 us (41%)
  matrix products  163 us (19%)
  local copies, waits for them, and re-layouts  160 us (18%)
  blocking collectives  81.2 us (9%)
  other arithmetic  66.1 us (8%)
  loops' own time  23.1 us (3%)
  starting transfers between devices  10.2 us (1%)
    ppermute x2, waiting for transfers between devices, shifted(): return lax.ppermute(shard, axis, pairs)  284 us
    all_to_all x1, blocking collectives, shards(): lax.all_to_all(split_kv, 'enc', split_axis=3, concat_axis=1, tiled=True)  81.2 us
    all_to_all x1, waiting for transfers between devices, shards(): lax.all_to_all(row_grads, 'enc', split_axis=1, concat_axis=3, tiled=True)  73.4 us
    dynamic_slice x98, local copies, waits for them, and re-layouts, forward_tiles(): lax.scan(online_step, starting_state, (head_keys, head_values, columns, a...  59.1 us
    dot_general x22, matrix products, score_block(): jnp.einsum('tgd,jd->tgj', query_head, key_tile, preferred_element_type=jn...  45.3 us
    squeeze x22, other arithmetic, forward_tiles(): lax.scan(online_step, starting_state, (head_keys, head_values, columns, a...  42 us
    dot_general x11, matrix products, online_update(): jnp.einsum('tgj,jd->tgd', probs.astype(jnp.bfloat16), value_tile, preferr...  35.2 us
    dot_general x11, matrix products, grad_update(): jnp.einsum('tgd,jd->tgj', grad_head, value_tile, preferred_element_type=j...  32.9 us
  transfers between devices with their start and end apart: 3, of which 3 were waited for; matrix products, arithmetic and copies ran while one was open for 0% of the time, Pallas kernels for 0%

commit v1 on v0

v1 whole, which is shorter than its diff:
```python
import functools

import jax
import jax.numpy as jnp
from jax import lax
from jax.experimental import pallas as pl
from jax.experimental.pallas import tpu as pltpu
from jax.sharding import PartitionSpec as P

HEAD = 128
SLOTS = 128
TILES = 4
GROUP = 8
ROWS = GROUP * SLOTS
NEG = -1e30
LOG2E = 1.4426950408889634
SCALE = HEAD**-0.5
NT = (((1,), (1,)), ((), ()))
NN = (((1,), (0,)), ((), ()))
BF = jnp.bfloat16
F32 = jnp.float32


def dot(a, b, dims=NN):
    return lax.dot_general(a, b, dims, preferred_element_type=F32)


def chunks(keys, size):
    padded = -(-keys // 128) * 128
    return padded, [(o, min(size, padded - o)) for o in range(0, padded, size)]


def head_rows(block):
    return jnp.concatenate([block[:, h * HEAD : (h + 1) * HEAD] for h in range(GROUP)], 0)


def split_tile(keys, kv_block, wide, k_pad, v_pad):
    padded = k_pad.shape[0]
    wide[0 : 2 * keys, :] = kv_block.reshape(2 * keys, HEAD).astype(F32)
    wide[2 * keys :, :] = jnp.zeros((2 * (padded - keys), HEAD), F32)
    k_pad[...] = wide[pl.ds(0, padded, 2), :].astype(BF)
    v_pad[...] = wide[pl.ds(1, padded, 2), :].astype(BF)


def forward_group(keys, k_pad, v_t, q, probs, scores, out_t):
    padded, parts = chunks(keys, 256)
    top = jnp.full((8, ROWS), NEG, F32)
    for o, n in parts:
        s = dot(k_pad[o : o + n, :], q, NT)
        if o + n > keys:
            s = jnp.where(lax.broadcasted_iota(jnp.int32, s.shape, 0) < keys - o, s, NEG)
        scores[o : o + n, :] = s
        top = jnp.maximum(top, jnp.max(s.reshape(n // 8, 8, ROWS), axis=0))
    top = jnp.max(top, axis=0, keepdims=True) * (SCALE * LOG2E)
    total = jnp.zeros((8, ROWS), F32)
    acc = jnp.zeros((HEAD, ROWS), F32)
    for o, n in parts:
        p = jnp.exp2(scores[o : o + n, :] * (SCALE * LOG2E) - top)
        total = total + jnp.sum(p.reshape(n // 8, 8, ROWS), axis=0)
        low = p.astype(BF)
        probs[o : o + n, :] = low
        acc = acc + dot(v_t[:, o : o + n], low)
    total = jnp.sum(total, axis=0, keepdims=True)
    out_t[...] = acc / total
    return top, top + jnp.log2(total)


def backward_group(keys, v_pad, k_t, q, g, probs, factor, delta, dq_t, wide):
    padded, parts = chunks(keys, 256)
    for o, n in parts:
        dp = dot(v_pad[o : o + n, :], g, NT)
        p = probs[o : o + n, :].astype(F32) * factor
        t = (p * (dp - delta)).astype(BF)
        wide[pl.ds(2 * o, n, 2), :] = dot(t, q) * SCALE
        wide[pl.ds(2 * o + 1, n, 2), :] = dot(p.astype(BF), g)
        d = dot(k_t[:, o : o + n], t)
        dq_t[...] = d if o == 0 else dq_t[...] + d


def forward_kernel(keys, q_ref, g_ref, kv_ref, p_ref, o_ref, stat_ref, wide, k_pad, v_pad, v_t, scores):
    split_tile(keys, kv_ref[...], wide, k_pad, v_pad)
    v_t[...] = v_pad[...].T
    top, lse = forward_group(keys, k_pad, v_t, head_rows(q_ref[...]), p_ref, scores, o_ref)
    for h in range(GROUP):
        lanes = slice(h * SLOTS, (h + 1) * SLOTS)
        g_t = g_ref[:, h * HEAD : (h + 1) * HEAD].T.astype(F32)
        stat_ref[0, h : h + 1, :] = top[:, lanes]
        stat_ref[1, h : h + 1, :] = lse[:, lanes]
        stat_ref[2, h : h + 1, :] = jnp.sum(o_ref[:, lanes] * g_t, axis=0, keepdims=True)


def backward_kernel(
    keys, q_ref, g_ref, kv_ref, p_ref, o_ref, stat_ref, out_ref, dkv_ref, wide, k_pad, v_pad, k_t, dq_t
):
    split_tile(keys, kv_ref[...], wide, k_pad, v_pad)
    k_t[...] = k_pad[...].T

    def lanes_of(i):
        return jnp.concatenate([stat_ref[i, h : h + 1, :] for h in range(GROUP)], 1)

    backward_group(
        keys,
        v_pad,
        k_t,
        head_rows(q_ref[...]),
        head_rows(g_ref[...]),
        p_ref,
        lanes_of(0),
        lanes_of(2),
        dq_t,
        wide,
    )
    dkv_ref[...] = wide[0 : 2 * keys, :].astype(BF).reshape(keys, 2, HEAD)
    share = lanes_of(1)
    for h in range(GROUP):
        lanes = slice(h * SLOTS, (h + 1) * SLOTS)
        cols = slice(h * HEAD, (h + 1) * HEAD)
        out_ref[0, :, cols] = (o_ref[:, lanes] * share[:, lanes]).T.astype(BF)
        out_ref[1, :, cols] = (dq_t[:, lanes] * SCALE).T.astype(BF)


def per_group(*shape):
    return pl.BlockSpec((None,) + shape, lambda g: (g,) + (0,) * len(shape))


def kv_spec(keys):
    return pl.BlockSpec((keys, None, 2, HEAD), lambda g: (0, g, 0, 0))


def run_forward(q, g, kv):
    keys = kv.shape[0]
    padded = chunks(keys, 256)[0]
    groups = kv.shape[1]
    return pl.pallas_call(
        functools.partial(forward_kernel, keys),
        grid=(groups,),
        out_shape=[
            jax.ShapeDtypeStruct((groups, padded, ROWS), BF),
            jax.ShapeDtypeStruct((groups, HEAD, ROWS), F32),
            jax.ShapeDtypeStruct((groups, 3, GROUP, SLOTS), F32),
        ],
        in_specs=[per_group(SLOTS, GROUP * HEAD)] * 2 + [kv_spec(keys)],
        out_specs=[per_group(padded, ROWS), per_group(HEAD, ROWS), per_group(3, GROUP, SLOTS)],
        scratch_shapes=[
            pltpu.VMEM((2 * padded, HEAD), F32),
            pltpu.VMEM((padded, HEAD), BF),
            pltpu.VMEM((padded, HEAD), BF),
            pltpu.VMEM((HEAD, padded), BF),
            pltpu.VMEM((padded, ROWS), F32),
        ],
        compiler_params=pltpu.CompilerParams(vmem_limit_bytes=48 * 2**20),
    )(q, g, kv)


def run_backward(q, g, kv, probs, out_t, stats):
    keys, groups = kv.shape[:2]
    padded = probs.shape[1]
    return pl.pallas_call(
        functools.partial(backward_kernel, keys),
        grid=(groups,),
        out_shape=[
            jax.ShapeDtypeStruct((groups, 2, SLOTS, GROUP * HEAD), BF),
            jax.ShapeDtypeStruct(kv.shape, BF),
        ],
        in_specs=[per_group(SLOTS, GROUP * HEAD)] * 2
        + [kv_spec(keys), per_group(padded, ROWS), per_group(HEAD, ROWS), per_group(3, GROUP, SLOTS)],
        out_specs=[per_group(2, SLOTS, GROUP * HEAD), kv_spec(keys)],
        scratch_shapes=[
            pltpu.VMEM((2 * padded, HEAD), F32),
            pltpu.VMEM((padded, HEAD), BF),
            pltpu.VMEM((padded, HEAD), BF),
            pltpu.VMEM((HEAD, padded), BF),
            pltpu.VMEM((HEAD, ROWS), F32),
        ],
        compiler_params=pltpu.CompilerParams(vmem_limit_bytes=48 * 2**20),
    )(q, g, kv, probs, out_t, stats)


def shifted(x, by):
    n = lax.axis_size("seq")
    return lax.ppermute(x, "seq", [(i, (i + by) % n) for i in range(n)])


def exchange(x):
    return lax.all_to_all(x, "enc", split_axis=0, concat_axis=0, tiled=True)


def slot_masks(spans, counts, row, groups):
    tiles = row * groups + jnp.arange(groups, dtype=jnp.int32)
    images = tiles // TILES
    used = (tiles - images * TILES) < counts[images]
    start, end = spans[images, 0], spans[images, 1]
    own = row * SLOTS + jnp.arange(SLOTS, dtype=jnp.int32)[None, :]
    later = own + SLOTS
    here = used[:, None] & (own >= start[:, None]) & (own < end[:, None])
    after = used[:, None] & (later >= start[:, None]) & (later < end[:, None])
    return here, after


def shards(queries, image_key_value, image_spans, tile_counts, cross_gate, grad_out):
    row = lax.axis_index("seq")
    tile = lax.axis_index("enc")
    rows, groups = lax.axis_size("seq"), lax.axis_size("enc")
    keys = image_key_value.shape[2]
    gate = jnp.tanh(cross_gate[0])
    grads = (gate * grad_out.astype(F32)).astype(BF)
    kv = image_key_value.reshape(2, keys, groups, HEAD).transpose(1, 2, 0, 3)

    images = row * (groups // TILES) + jnp.arange(groups // TILES, dtype=jnp.int32)
    starts = image_spans[images, 0]
    own = (row * SLOTS + jnp.arange(SLOTS, dtype=jnp.int32))[None, :] >= starts[:, None]

    def gathered(x):
        y = jnp.where(own[:, :, None], x[None], shifted(x, -1)[None])
        return exchange(jnp.repeat(y, TILES, axis=0))

    q_all, g_all = gathered(queries), gathered(grads)
    probs, out_t, stats = run_forward(q_all, g_all, kv)

    here, after = slot_masks(image_spans, tile_counts, row, groups)
    here_before, after_before = slot_masks(image_spans, tile_counts, (row - 1) % rows, groups)
    here_next, after_next = slot_masks(image_spans, tile_counts, (row + 1) % rows, groups)
    mine = exchange(stats[:, 1:])
    before, later = shifted(mine, 1), shifted(mine, -1)

    def combined(a, a_mask, b, b_mask):
        lse = jnp.concatenate([a[:, 0], b[:, 0]], 0)
        lse = jnp.where(jnp.concatenate([a_mask, b_mask], 0)[:, None, :], lse, NEG)
        delta = jnp.concatenate([a[:, 1], b[:, 1]], 0)
        top = jnp.max(lse, axis=0)
        part = jnp.exp2(lse - top)
        part = jnp.where(lse > 0.5 * NEG, part, 0.0)
        total = jnp.sum(part, axis=0)
        safe = jnp.where(total > 0.0, total, 1.0)
        return top + jnp.log2(safe), jnp.sum(part * delta, axis=0) / safe

    lse_here, delta_here = combined(mine, here, before, after_before)
    lse_after, delta_after = combined(later, here_next, mine, after)
    pick = own[:, None, :]
    final = jnp.stack(
        [jnp.where(pick, lse_here, lse_after), jnp.where(pick, delta_here, delta_after)], 1
    )
    final = exchange(jnp.repeat(final, TILES, axis=0))
    valid = (here | after)[tile][None, None, :]
    factor = jnp.where(valid, jnp.exp2(stats[:, 0] - final[:, 0]), 0.0)
    share = jnp.where(valid, jnp.exp2(stats[:, 1] - final[:, 0]), 0.0)
    parts, dkv = run_backward(
        q_all, g_all, kv, probs, out_t, jnp.stack([factor, share, final[:, 1]], 1)
    )
    parts = exchange(parts).astype(F32)
    sums = parts.reshape(groups // TILES, TILES, 2, SLOTS, GROUP * HEAD).sum(1)
    at_own = own[:, None, :, None]
    stay = jnp.where(at_own, sums, 0.0).sum(0)
    leave = jnp.where(at_own, 0.0, sums).sum(0).astype(BF)
    total = stay + shifted(leave, 1).astype(F32)
    attended = (gate * total[0]).astype(BF)
    grad_queries = total[1].astype(BF)
    grad_image_kv = dkv.transpose(2, 0, 1, 3).reshape(2, 1, keys, groups * HEAD)
    return attended, grad_queries, grad_image_kv


def solution(mesh):
    kv_part = P(None, ("seq", "enc"), None, None)
    return jax.shard_map(
        shards,
        mesh=mesh,
        in_specs=(P("seq", "enc"), kv_part, P(), P(), P(), P("seq", "enc")),
        out_specs=(P("seq", "enc"), P("seq", "enc"), kv_part),
        check_vma=False,
    )
```

time: 867 us -> 259 us (0.30)
  the two profiles are of different devices: /device:TPU:4 before, /device:TPU:1 now
where the time goes in v1:
time: 259 us; the launch traced here: 258 us
  waiting for transfers between devices  83.5 us (32%)
  Pallas kernels  69.8 us (27%)
  blocking collectives  53.7 us (21%)
  starting transfers between devices  32.8 us (13%)
  local copies, waits for them, and re-layouts  11.8 us (5%)
  other arithmetic  5.1 us (2%)
    all_to_all x4, waiting for transfers between devices, exchange(): return lax.all_to_all(x, 'enc', split_axis=0, concat_axis=0, tiled=True)  56.1 us
    all_to_all x1, blocking collectives, exchange(): return lax.all_to_all(x, 'enc', split_axis=0, concat_axis=0, tiled=True)  53.7 us
    pallas_call x1, Pallas kernels, run_backward(): pl.pallas_call(functools.partial(backward_kernel, keys), grid=(groups,),...  37.8 us
    pallas_call x1, Pallas kernels, run_forward(): pl.pallas_call(functools.partial(forward_kernel, keys), grid=(groups,), o...  32 us
    ppermute x5, waiting for transfers between devices, shifted(): return lax.ppermute(x, 'seq', [(i, (i + by) % n) for i in range(n)])  27.4 us
    all_to_all x4, starting transfers between devices, exchange(): return lax.all_to_all(x, 'enc', split_axis=0, concat_axis=0, tiled=True)  21 us
    ppermute x5, starting transfers between devices, shifted(): return lax.ppermute(x, 'seq', [(i, (i + by) % n) for i in range(n)])  11.8 us
  transfers between devices with their start and end apart: 9, of which 8 were waited for; matrix products, arithmetic and copies ran while one was open for 3% of the time, Pallas kernels for 0%

profile of v1, /device:TPU:1, one launch (start us, length us, event | category | flops | bytes accessed | tf_op | source)
XLA Modules:
  0.0 258.2 jit_solution(9082493009183668981)
XLA Ops:
  1.3 1.0 multiply_convert_fusion
  2.4 5.8 %collective-permute-start.1 = (bf16[128,1024]{1,0:T(8,128)(2,1)S(1)}, bf16[128,1024]{1,0:T(8,128)(2,1)S(1)}, u32[]{:S(2)}, u32[]{:S(2)}) collective-permute-start(bf16[128,1024]{1,0:T(8,128)(2,1)S(1)} %multiply_convert_fusion), channel_id=1, source_target_pairs={{0,120},{8,0},{16,8},{24,16},{32,24},{40,32},{48,40},{56,48},{64,5... | collective-permute-start | bytes 786440 | tf_op jit(solution)/shard_map/ppermute | solution.py:181
  9.4 3.8 %collective-permute-done.1 = bf16[128,1024]{1,0:T(8,128)(2,1)S(1)} collective-permute-done((bf16[128,1024]{1,0:T(8,128)(2,1)S(1)}, bf16[128,1024]{1,0:T(8,128)(2,1)S(1)}, u32[]{:S(2)}, u32[]{:S(2)}) %collective-permute-start.1) | collective-permute-done | bytes 262176 | tf_op jit(solution)/shard_map/ppermute | solution.py:181
  13.2 5.7 %collective-permute-done = bf16[128,1024]{1,0:T(8,128)(2,1)S(1)} collective-permute-done((bf16[128,1024]{1,0:T(8,128)(2,1)}, bf16[128,1024]{1,0:T(8,128)(2,1)S(1)}, u32[]{:S(2)}, u32[]{:S(2)}) %collective-permute-start) | collective-permute-done | bytes 262176 | tf_op jit(solution)/shard_map/ppermute | solution.py:181
  18.9 1.1 broadcast_select_fusion
  20.0 1.6 broadcast_in_dim.183
  21.6 6.9 %all-to-all-start.1 = ((bf16[8,128,1024]{2,1,0:T(8,128)(2,1)}), bf16[8,128,1024]{2,1,0:T(8,128)(2,1)S(1)}, u32[]{:S(2)}, u32[]{:S(2)}) async-start(bf16[8,128,1024]{2,1,0:T(8,128)(2,1)} %bitcast.54), calls=%async_computation.1 | async-start | bytes 4194304 | tf_op jit(solution)/shard_map/all_to_all | solution.py:185
  28.6 26.2 %all-to-all-done.1.g_ref = bf16[8,128,1024]{2,1,0:T(8,128)(2,1)S(1)} async-done(((bf16[8,128,1024]{2,1,0:T(8,128)(2,1)}), bf16[8,128,1024]{2,1,0:T(8,128)(2,1)S(1)}, u32[]{:S(2)}, u32[]{:S(2)}) %all-to-all-start.1) | async-done | bytes 2097184 | tf_op jit(solution)/shard_map/all_to_all | solution.py:185
  54.8 1.6 broadcast_in_dim.180
  56.4 5.1 %all-to-all-start = ((bf16[8,128,1024]{2,1,0:T(8,128)(2,1)}), bf16[8,128,1024]{2,1,0:T(8,128)(2,1)}, u32[]{:S(2)}, u32[]{:S(2)}) async-start(bf16[8,128,1024]{2,1,0:T(8,128)(2,1)} %bitcast.53), calls=%async_computation | async-start | bytes 4194304 | tf_op jit(solution)/shard_map/all_to_all | solution.py:185
  61.5 0.7 gather_fusion.2
  62.2 0.7 gather_fusion.5
  62.8 0.7 gather_fusion.8
  63.5 0.7 gather_fusion.3
  64.1 0.7 gather_fusion.6
  64.8 0.7 gather_fusion.9
  65.5 0.7 gather_fusion.7
  66.1 0.6 gather_fusion.4
  67.7 20.2 %all-to-all-done.q_ref = bf16[8,128,1024]{2,1,0:T(8,128)(2,1)} async-done(((bf16[8,128,1024]{2,1,0:T(8,128)(2,1)}), bf16[8,128,1024]{2,1,0:T(8,128)(2,1)}, u32[]{:S(2)}, u32[]{:S(2)}) %all-to-all-start) | async-done | bytes 2097184 | tf_op jit(solution)/shard_map/all_to_all | solution.py:185
  88.0 32.0 %shard_map.85 = (bf16[8,1664,1024]{2,1,0:T(8,128)(2,1)}, f32[8,128,1024]{2,1,0:T(8,128)}, f32[8,3,8,128]{3,2,1,0:T(8,128)S(1)}) custom-call(bf16[8,128,1024]{2,1,0:T(8,128)(2,1)} %all-to-all-done.q_ref, bf16[8,128,1024]{2,1,0:T(8,128)(2,1)S(1)} %all-to-all-done.1.g_ref, bf16[1601,8,2,128]{3,2,1,0:T(2,128)(2,1)} %bitcast.51), custom_call_target="tpu_custom_call" | custom-call | tf_op jit(solution)/shard_map/pallas_call | solution.py:134
  120.6 4.1 %all-to-all-start.2 = ((f32[8,2,8,128]{3,2,1,0:T(8,128)}), f32[8,2,8,128]{3,2,1,0:T(8,128)S(1)}, u32[]{:S(2)}, u32[]{:S(2)}) async-start(f32[8,2,8,128]{3,2,1,0:T(8,128)} %slice.44), calls=%async_computation.2 | async-start | bytes 131072 | tf_op jit(solution)/shard_map/all_to_all | solution.py:185
  124.7 4.9 %all-to-all-done.2 = f32[8,2,8,128]{3,2,1,0:T(8,128)S(1)} async-done(((f32[8,2,8,128]{3,2,1,0:T(8,128)}), f32[8,2,8,128]{3,2,1,0:T(8,128)S(1)}, u32[]{:S(2)}, u32[]{:S(2)}) %all-to-all-start.2) | async-done | bytes 65568 | tf_op jit(solution)/shard_map/all_to_all | solution.py:185
  129.6 5.5 %collective-permute-start.3 = (f32[8,2,8,128]{3,2,0,1:T(8,128)S(1)}, f32[8,2,8,128]{3,2,0,1:T(8,128)S(1)}, u32[]{:S(2)}, u32[]{:S(2)}) collective-permute-start(f32[8,2,8,128]{3,2,0,1:T(8,128)S(1)} %copy.15), channel_id=1, source_target_pairs={{0,120},{8,0},{16,8},{24,16},{32,24},{40,32},{48,40},{56,48},{64,5... | collective-permute-start | bytes 196616 | tf_op jit(solution)/shard_map/ppermute | solution.py:181
  135.1 1.6 collective-permute-done.2
  137.5 4.9 %all-to-all-start.3 = ((f32[8,2,8,128]{3,2,1,0:T(8,128)}), f32[8,2,8,128]{3,2,1,0:T(8,128)S(1)}, u32[]{:S(2)}, u32[]{:S(2)}) async-start(f32[8,2,8,128]{3,2,1,0:T(8,128)} %bitcast.23), calls=%async_computation.3 | async-start | bytes 131072 | tf_op jit(solution)/shard_map/all_to_all | solution.py:185
  142.4 4.9 %all-to-all-done.3 = f32[8,2,8,128]{3,2,1,0:T(8,128)S(1)} async-done(((f32[8,2,8,128]{3,2,1,0:T(8,128)}), f32[8,2,8,128]{3,2,1,0:T(8,128)S(1)}, u32[]{:S(2)}, u32[]{:S(2)}) %all-to-all-start.3) | async-done | bytes 65568 | tf_op jit(solution)/shard_map/all_to_all | solution.py:185
  147.3 37.8 %shard_map.86 = (bf16[8,2,128,1024]{3,2,1,0:T(8,128)(2,1)}, bf16[1601,8,2,128]{3,2,1,0:T(2,128)(2,1)}) custom-call(bf16[8,128,1024]{2,1,0:T(8,128)(2,1)} %all-to-all-done.q_ref, bf16[8,128,1024]{2,1,0:T(8,128)(2,1)S(1)} %all-to-all-done.1.g_ref, bf16[1601,8,2,128]{3,2,1,0:T(2,128)(2,1)} %bitcast.52, bf16[8,1664,1024]{2,1,0:T(8,128)(2,1)} %get-tuple-element.8.p_ref, ...), custom_call_target="tpu_custom_call" | custom-call | tf_op jit(solution)/shard_map/pallas_call | solution.py:158
  185.1 53.7 %all_to_all.25 = bf16[8,2,128,1024]{3,2,1,0:T(8,128)(2,1)S(1)} all-to-all(bf16[8,2,128,1024]{3,2,1,0:T(8,128)(2,1)} %get-tuple-element.11), channel_id=1, replica_groups=mesh['seq'=16,'enc'=8] {'enc'}, dimensions={0} | all-to-all | bytes 8388608 | tf_op jit(solution)/shard_map/all_to_all | solution.py:185
  238.7 0.9 convert_reduce_fusion
  240.3 16.3 %collective-permute-done.4 = bf16[2,128,1024]{2,1,0:T(8,128)(2,1)S(1)} collective-permute-done((bf16[2,128,1024]{2,1,0:T(8,128)(2,1)S(1)}, bf16[2,128,1024]{2,1,0:T(8,128)(2,1)S(1)}, u32[]{:S(2)}, u32[]{:S(2)}) %collective-permute-start.4) | collective-permute-done | bytes 524320 | tf_op jit(solution)/shard_map/ppermute | solution.py:181
  256.7 0.7 fusion.1
  257.5 0.7 fusion.2
  (53 shorter events, 4.5 us)
Async XLA Ops:
  0.6 8.0 %copy-start = (s32[32,2]{0,1:T(2,128)S(1)}, s32[32,2]{0,1:T(2,128)}, u32[]{:S(2)}) copy-start(s32[32,2]{0,1:T(2,128)} %param.8) | copy-start | bytes 772
  2.4 10.8 %collective-permute-start.1 = (bf16[128,1024]{1,0:T(8,128)(2,1)S(1)}, bf16[128,1024]{1,0:T(8,128)(2,1)S(1)}, u32[]{:S(2)}, u32[]{:S(2)}) collective-permute-start(bf16[128,1024]{1,0:T(8,128)(2,1)S(1)} %multiply_convert_fusion), channel_id=1, source_target_pairs={{0,120},{8,0},{16,8},{24,16},{32,24},{40,32},{48,40},{56,48},{64,5... | collective-permute-start | bytes 786440 | tf_op jit(solution)/shard_map/ppermute | solution.py:181
  8.2 10.7 %collective-permute-start = (bf16[128,1024]{1,0:T(8,128)(2,1)}, bf16[128,1024]{1,0:T(8,128)(2,1)S(1)}, u32[]{:S(2)}, u32[]{:S(2)}) collective-permute-start(bf16[128,1024]{1,0:T(8,128)(2,1)} %param.6), channel_id=1, source_target_pairs={{0,120},{8,0},{16,8},{24,16},{32,24},{40,32},{48,40},{56,48},{64,5... | collective-permute-start | bytes 786440 | tf_op jit(solution)/shard_map/ppermute | solution.py:181
  21.6 33.2 %all-to-all-start.1 = ((bf16[8,128,1024]{2,1,0:T(8,128)(2,1)}), bf16[8,128,1024]{2,1,0:T(8,128)(2,1)S(1)}, u32[]{:S(2)}, u32[]{:S(2)}) async-start(bf16[8,128,1024]{2,1,0:T(8,128)(2,1)} %bitcast.54), calls=%async_computation.1 | async-start | bytes 4194304 | tf_op jit(solution)/shard_map/all_to_all | solution.py:185
  56.4 31.6 %all-to-all-start = ((bf16[8,128,1024]{2,1,0:T(8,128)(2,1)}), bf16[8,128,1024]{2,1,0:T(8,128)(2,1)}, u32[]{:S(2)}, u32[]{:S(2)}) async-start(bf16[8,128,1024]{2,1,0:T(8,128)(2,1)} %bitcast.53), calls=%async_computation | async-start | bytes 4194304 | tf_op jit(solution)/shard_map/all_to_all | solution.py:185
  61.5 4.0 %copy-start.2 = (s32[32]{0:T(128)S(1)}, s32[32]{0:T(128)}, u32[]{:S(2)}) copy-start(s32[32]{0:T(128)} %param.9) | copy-start | bytes 388
  120.6 9.0 %all-to-all-start.2 = ((f32[8,2,8,128]{3,2,1,0:T(8,128)}), f32[8,2,8,128]{3,2,1,0:T(8,128)S(1)}, u32[]{:S(2)}, u32[]{:S(2)}) async-start(f32[8,2,8,128]{3,2,1,0:T(8,128)} %slice.44), calls=%async_computation.2 | async-start | bytes 131072 | tf_op jit(solution)/shard_map/all_to_all | solution.py:185
  129.6 7.1 %collective-permute-start.2 = (f32[8,2,8,128]{3,2,0,1:T(8,128)S(1)}, f32[8,2,8,128]{3,2,0,1:T(8,128)S(1)}, u32[]{:S(2)}, u32[]{:S(2)}) collective-permute-start(f32[8,2,8,128]{3,2,0,1:T(8,128)S(1)} %copy.15), channel_id=1, source_target_pairs={{0,8},{8,16},{16,24},{24,32},{32,40},{40,48},{48,56},{56,64},{64,7... | collective-permute-start | bytes 196616 | tf_op jit(solution)/shard_map/ppermute | solution.py:181
  129.6 7.1 %collective-permute-start.3 = (f32[8,2,8,128]{3,2,0,1:T(8,128)S(1)}, f32[8,2,8,128]{3,2,0,1:T(8,128)S(1)}, u32[]{:S(2)}, u32[]{:S(2)}) collective-permute-start(f32[8,2,8,128]{3,2,0,1:T(8,128)S(1)} %copy.15), channel_id=1, source_target_pairs={{0,120},{8,0},{16,8},{24,16},{32,24},{40,32},{48,40},{56,48},{64,5... | collective-permute-start | bytes 196616 | tf_op jit(solution)/shard_map/ppermute | solution.py:181
  137.5 9.8 %all-to-all-start.3 = ((f32[8,2,8,128]{3,2,1,0:T(8,128)}), f32[8,2,8,128]{3,2,1,0:T(8,128)S(1)}, u32[]{:S(2)}, u32[]{:S(2)}) async-start(f32[8,2,8,128]{3,2,1,0:T(8,128)} %bitcast.23), calls=%async_computation.3 | async-start | bytes 131072 | tf_op jit(solution)/shard_map/all_to_all | solution.py:185
  239.7 18.6 %copy-start.1 = (s32[32,2]{0,1:T(2,128)S(1)}, s32[32,2]{0,1:T(2,128)}, u32[]{:S(2)}) copy-start(s32[32,2]{0,1:T(2,128)} %param.8) | copy-start | bytes 772
  240.2 16.4 %collective-permute-start.4 = (bf16[2,128,1024]{2,1,0:T(8,128)(2,1)S(1)}, bf16[2,128,1024]{2,1,0:T(8,128)(2,1)S(1)}, u32[]{:S(2)}, u32[]{:S(2)}) collective-permute-start(bf16[2,128,1024]{2,1,0:T(8,128)(2,1)S(1)} %get-tuple-element.13), channel_id=1, source_target_pairs={{0,8},{8,16},{16,24},{24,32},{32,40},{40,48},{48,56},{56,64},{64,7... | collective-permute-start | bytes 1572872 | tf_op jit(solution)/shard_map/ppermute | solution.py:181

commit v2 on v1

v2 whole, which is shorter than its diff:
```python
import functools

import jax
import jax.numpy as jnp
from jax import lax
from jax.experimental import pallas as pl
from jax.experimental.pallas import tpu as pltpu
from jax.sharding import PartitionSpec as P

HEAD = 128
SLOTS = 128
TILES = 4
GROUP = 8
ROWS = GROUP * SLOTS
NEG = -1e30
LOG2E = 1.4426950408889634
SCALE = HEAD**-0.5
NT = (((1,), (1,)), ((), ()))
NN = (((1,), (0,)), ((), ()))
BF = jnp.bfloat16
F32 = jnp.float32


def dot(a, b, dims=NN):
    return lax.dot_general(a, b, dims, preferred_element_type=F32)


def chunks(keys, size):
    padded = -(-keys // 128) * 128
    return padded, [(o, min(size, padded - o)) for o in range(0, padded, size)]


def head_rows(block):
    return jnp.concatenate([block[:, h * HEAD : (h + 1) * HEAD] for h in range(GROUP)], 0)


def split_tile(keys, kv_block, wide, k_pad, v_pad):
    padded = k_pad.shape[0]
    wide[0 : 2 * keys, :] = kv_block.reshape(2 * keys, HEAD).astype(F32)
    wide[2 * keys :, :] = jnp.zeros((2 * (padded - keys), HEAD), F32)
    k_pad[...] = wide[pl.ds(0, padded, 2), :].astype(BF)
    v_pad[...] = wide[pl.ds(1, padded, 2), :].astype(BF)


def forward_group(keys, k_pad, v_t, q, probs, scores, out_t):
    padded, parts = chunks(keys, 256)
    top = jnp.full((8, ROWS), NEG, F32)
    for o, n in parts:
        s = dot(k_pad[o : o + n, :], q, NT)
        if o + n > keys:
            s = jnp.where(lax.broadcasted_iota(jnp.int32, s.shape, 0) < keys - o, s, NEG)
        scores[o : o + n, :] = s
        top = jnp.maximum(top, jnp.max(s.reshape(n // 8, 8, ROWS), axis=0))
    top = jnp.max(top, axis=0, keepdims=True) * (SCALE * LOG2E)
    total = jnp.zeros((8, ROWS), F32)
    acc = jnp.zeros((HEAD, ROWS), F32)
    for o, n in parts:
        p = jnp.exp2(scores[o : o + n, :] * (SCALE * LOG2E) - top)
        total = total + jnp.sum(p.reshape(n // 8, 8, ROWS), axis=0)
        low = p.astype(BF)
        probs[o : o + n, :] = low
        acc = acc + dot(v_t[:, o : o + n], low)
    total = jnp.sum(total, axis=0, keepdims=True)
    out_t[...] = acc / total
    return top, top + jnp.log2(total)


def backward_group(keys, v_pad, k_t, q, g, probs, factor, delta, dq_t, wide):
    padded, parts = chunks(keys, 256)
    for o, n in parts:
        dp = dot(v_pad[o : o + n, :], g, NT)
        p = probs[o : o + n, :].astype(F32) * factor
        t = (p * (dp - delta)).astype(BF)
        wide[pl.ds(2 * o, n, 2), :] = dot(t, q) * SCALE
        wide[pl.ds(2 * o + 1, n, 2), :] = dot(p.astype(BF), g)
        d = dot(k_t[:, o : o + n], t)
        dq_t[...] = d if o == 0 else dq_t[...] + d


MESH = pl.DeviceIdType.MESH


def merged(entries):
    top = entries[0][0]
    for lse, _ in entries[1:]:
        top = jnp.maximum(top, lse)
    total = jnp.zeros_like(top)
    mean = jnp.zeros_like(top)
    for lse, delta in entries:
        part = jnp.where(lse > 0.5 * NEG, jnp.exp2(lse - top), 0.0)
        total = total + part
        mean = mean + part * delta
    seen = total > 0.0
    safe = jnp.where(seen, total, 1.0)
    return jnp.where(seen, top + jnp.log2(safe), NEG), mean / safe


def step_kernel(
    keys,
    q_ref,
    g_ref,
    kv_ref,
    spans,
    counts,
    gate_ref,
    attended_ref,
    dq_ref,
    dkv_ref,
    g_low,
    next_q,
    next_g,
    pick_q,
    pick_g,
    q_all,
    g_all,
    kv_buf,
    dkv_buf,
    wide,
    k_pad,
    v_pad,
    turned,
    scores,
    probs,
    out_t,
    dq_t,
    tops,
    stat_out,
    stat_in,
    seq_out,
    seq_in,
    fin_out,
    fin_in,
    weight,
    o_out,
    o_in,
    d_out,
    d_in,
    stay,
    leave,
    arrived,
    kv_sem,
    dkv_sem,
    next_send,
    next_recv,
    q_send,
    q_recv,
    g_send,
    g_recv,
    stat_send,
    stat_recv,
    seq_send,
    seq_recv,
    fin_send,
    fin_recv,
    o_send,
    o_recv,
    d_send,
    d_recv,
    leave_send,
    leave_recv,
):
    row = lax.axis_index("seq")
    me = lax.axis_index("enc")
    rows = lax.axis_size("seq")
    groups = lax.axis_size("enc")
    chips = groups // 2
    z, core = me // 2, me % 2
    other = me + 1 - 2 * core
    image = me // TILES
    above, below = (row + 1) % rows, (row + rows - 1) % rows

    def remote(src, dst, send, recv, to):
        return pltpu.make_async_remote_copy(
            src_ref=src, dst_ref=dst, send_sem=send, recv_sem=recv, device_id=to, device_id_type=MESH
        )

    def group_at(i):
        j = i // 2
        hop = j + j // 2 - 2 * (j // 3)
        return 2 * ((z + hop) % chips) + (core + i) % 2

    def kv_load(g, slot):
        return pltpu.make_async_copy(kv_ref.at[:, g], kv_buf.at[slot, 0:keys], kv_sem.at[slot])

    def dkv_store(g, slot):
        return pltpu.make_async_copy(dkv_buf.at[slot, 0:keys], dkv_ref.at[:, g], dkv_sem.at[slot])

    kv_load(group_at(0), 0).start()

    barrier = pltpu.get_barrier_semaphore()
    for j in range(1, groups):
        pl.semaphore_signal(barrier, inc=1, device_id=(row, (me + j) % groups), device_id_type=MESH)
    for r in (above, below):
        pl.semaphore_signal(barrier, inc=1, device_id=(r, me), device_id_type=MESH)
    pl.semaphore_wait(barrier, groups + 1)

    to_below = (below, me)
    send_q = remote(q_ref, next_q, next_send.at[0], next_recv.at[0], to_below)
    send_q.start()
    gate = jnp.tanh(jnp.full((SLOTS, HEAD), gate_ref[0], F32))
    for h in range(GROUP):
        cols = slice(h * HEAD, (h + 1) * HEAD)
        g_low[:, cols] = (gate * g_ref[:, cols].astype(F32)).astype(BF)
    send_g = remote(g_low, next_g, next_send.at[1], next_recv.at[1], to_below)
    send_g.start()

    starts = [spans[2 * row + i, 0] for i in range(2)]
    ends = [spans[2 * row + i, 1] for i in range(2)]
    used = [counts[2 * row + i] for i in range(2)]
    at_rows = row * SLOTS + lax.broadcasted_iota(jnp.int32, (SLOTS, HEAD), 0)
    at_lanes = row * SLOTS + lax.broadcasted_iota(jnp.int32, (GROUP, SLOTS), 1)
    own_rows = [at_rows >= starts[i] for i in range(2)]
    own_lanes = [at_lanes >= starts[i] for i in range(2)]

    def fan_out(mine, later, picked, everywhere, send, recv):
        for h in range(GROUP):
            cols = slice(h * HEAD, (h + 1) * HEAD)
            a, b = mine[:, cols].astype(F32), later[:, cols].astype(F32)
            for i in range(2):
                picked[i, :, cols] = jnp.where(own_rows[i], a, b).astype(BF)
        everywhere[me] = picked[image]
        remote(picked.at[image], everywhere.at[me], send.at[0], recv.at[me], (row, other)).start()
        for n, hop in enumerate((1, chips - 1, 2)):
            peer = 2 * ((z + hop) % chips) + core
            remote(
                picked.at[peer // TILES], everywhere.at[me], send.at[1 + n], recv.at[me], (row, peer)
            ).start()

    def arrival(buf, send, recv, g):
        return remote(buf.at[g], buf.at[g], send.at[0], recv.at[g], (row, other))

    def hand_on(buf, send, recv, i, n):
        g = group_at(i)
        return remote(buf.at[g], buf.at[g], send.at[n], recv.at[g], (row, other))

    send_q.wait_recv()
    fan_out(q_ref, next_q, pick_q, q_all, q_send, q_recv)
    send_g.wait_recv()
    fan_out(g_low, next_g, pick_g, g_all, g_send, g_recv)

    def forward(i, carry):
        g = group_at(i)
        slot = i % 2
        kv_load(g, slot).wait()
        kv_load(group_at(jnp.minimum(i + 1, groups - 1)), 1 - slot).start()

        @pl.when(i > 0)
        def _():
            arrival(q_all, q_send, q_recv, g).wait_recv()

        for n in range(3):
            @pl.when(i == 2 + 2 * n)
            def _():
                hand_on(q_all, q_send, q_recv, 2 + 2 * n, 4 + n).start()

            @pl.when(i == 5 + n)
            def _():
                arrival(g_all, g_send, g_recv, group_at(2 + 2 * n)).wait_recv()
                hand_on(g_all, g_send, g_recv, 2 + 2 * n, 4 + n).start()

        split_tile(keys, kv_buf[slot, 0:keys], wide, k_pad, v_pad)
        turned[...] = v_pad[...].T
        top, lse = forward_group(
            keys, k_pad, turned, head_rows(q_all[g]), probs.at[g], scores, out_t.at[g]
        )
        for h in range(GROUP):
            lanes = slice(h * SLOTS, (h + 1) * SLOTS)
            tops[g, h : h + 1, :] = top[:, lanes]
            stat_out[g, 0, h : h + 1, :] = lse[:, lanes]
        return carry

    lax.fori_loop(0, groups, forward, 0)

    def stat_copy(g, n):
        return remote(stat_out.at[g], stat_in.at[me], stat_send.at[n], stat_recv.at[me], (row, g))

    def delta(i, carry):
        g = group_at(i)

        @pl.when(i % 2 == 1)
        def _():
            arrival(g_all, g_send, g_recv, g).wait_recv()

        for h in range(GROUP):
            lanes = slice(h * SLOTS, (h + 1) * SLOTS)
            g_t = g_all[g, :, h * HEAD : (h + 1) * HEAD].T.astype(F32)
            stat_out[g, 1, h : h + 1, :] = jnp.sum(out_t[g, :, lanes] * g_t, axis=0, keepdims=True)

        @pl.when(i > 0)
        def _():
            stat_copy(g, i).start()

        return carry

    lax.fori_loop(0, groups, delta, 0)
    stat_in[me] = stat_out[me]
    for j in range(1, groups):
        src = (me + j) % groups
        remote(stat_out.at[0], stat_in.at[src], stat_send.at[0], stat_recv.at[src], (row, src)).wait_recv()

    def seen(c, shift):
        i = c // TILES
        end = jnp.where(c % TILES < used[i], ends[i], 0)
        at = at_lanes + shift
        return (at >= starts[i]) & (at < end)

    here, after = [], []
    for c in range(2 * TILES):
        lse, mean = stat_in[c, 0], stat_in[c, 1]
        here.append((jnp.where(seen(c, 0), lse, NEG), mean))
        after.append((jnp.where(seen(c, SLOTS), lse, NEG), mean))
    here, after = merged(here), merged(after)
    seq_out[0, 0], seq_out[0, 1] = after
    seq_out[1, 0], seq_out[1, 1] = here
    up = remote(seq_out.at[0], seq_in.at[0], seq_send.at[0], seq_recv.at[0], (above, me))
    down = remote(seq_out.at[1], seq_in.at[1], seq_send.at[1], seq_recv.at[1], (below, me))
    up.start()
    down.start()
    up.wait_recv()
    down.wait_recv()
    here = merged([here, (seq_in[0, 0], seq_in[0, 1])])
    after = merged([after, (seq_in[1, 0], seq_in[1, 1])])
    for i in range(2):
        for n in range(2):
            fin_out[i, n] = jnp.where(own_lanes[i], here[n], after[n])
    fin_in[me] = fin_out[image]
    for j in range(1, groups):
        c = (me + j) % groups
        remote(fin_out.at[c // TILES], fin_in.at[me], fin_send.at[j], fin_recv.at[me], (row, c)).start()

    my_used = counts[2 * row + image]
    my_start = spans[2 * row + image, 0]
    my_end = jnp.where(me % TILES < my_used, spans[2 * row + image, 1], 0)
    shown = ((at_lanes >= my_start) & (at_lanes < my_end)) | (
        (at_lanes + SLOTS >= my_start) & (at_lanes + SLOTS < my_end)
    )

    def part_copy(out, dest, send, recv, g, n):
        return remote(out.at[g], dest.at[me], send.at[n], recv.at[me], (row, g))

    def settle(out, dest, recv, send, n, result):
        for j in range(1, groups):
            src = (me + j) % groups
            remote(out.at[0], dest.at[src], send.at[0], recv.at[src], (row, src)).wait_recv()
        dest[me] = out[me]
        for h in range(GROUP):
            cols = slice(h * HEAD, (h + 1) * HEAD)
            sums = []
            for i in range(2):
                total = dest[TILES * i, :, cols].astype(F32)
                for c in range(1, TILES):
                    total = total + dest[TILES * i + c, :, cols].astype(F32)
                sums.append(total)
            kept = [jnp.where(own_rows[i], sums[i], 0.0) for i in range(2)]
            gone = [jnp.where(own_rows[i], 0.0, sums[i]) for i in range(2)]
            stay[n, :, cols] = kept[0] + kept[1]
            leave[n, :, cols] = (gone[0] + gone[1]).astype(BF)
        leave_copy(n).start()

    def leave_copy(n):
        return remote(leave.at[n], arrived.at[n], leave_send.at[n], leave_recv.at[n], (above, me))

    def backward(i, carry):
        g = group_at(groups - 1 - i)
        slot = i % 2
        kv_load(g, slot).wait()

        @pl.when(i < groups - 1)
        def _():
            kv_load(group_at(groups - 2 - i), 1 - slot).start()
            remote(fin_out.at[0], fin_in.at[g], fin_send.at[0], fin_recv.at[g], (row, g)).wait_recv()

        lse, mean = fin_in[g, 0], fin_in[g, 1]
        weight[0] = jnp.where(shown, jnp.exp2(tops[g] - lse), 0.0)
        weight[1] = jnp.where(shown, jnp.exp2(stat_out[g, 0] - lse), 0.0)
        weight[2] = mean

        def lanes_of(n):
            return jnp.concatenate([weight[n, h : h + 1, :] for h in range(GROUP)], 1)

        for h in range(GROUP):
            lanes = slice(h * SLOTS, (h + 1) * SLOTS)
            cols = slice(h * HEAD, (h + 1) * HEAD)
            o_out[g, :, cols] = (out_t[g, :, lanes] * weight[1, h : h + 1, :]).T.astype(BF)

        @pl.when(i < groups - 1)
        def _():
            part_copy(o_out, o_in, o_send, o_recv, g, i).start()

        @pl.when(i == groups - 1)
        def _():
            settle(o_out, o_in, o_recv, o_send, 0, attended_ref)

        @pl.when(i >= 2)
        def _():
            dkv_store(g, slot).wait()

        split_tile(keys, kv_buf[slot, 0:keys], wide, k_pad, v_pad)
        turned[...] = k_pad[...].T
        backward_group(
            keys,
            v_pad,
            turned,
            head_rows(q_all[g]),
            head_rows(g_all[g]),
            probs.at[g],
            lanes_of(0),
            lanes_of(2),
            dq_t,
            wide,
        )
        for h in range(GROUP):
            lanes = slice(h * SLOTS, (h + 1) * SLOTS)
            cols = slice(h * HEAD, (h + 1) * HEAD)
            d_out[g, :, cols] = (dq_t[:, lanes] * SCALE).T.astype(BF)

        @pl.when(i < groups - 1)
        def _():
            part_copy(d_out, d_in, d_send, d_recv, g, i).start()

        dkv_buf[slot, 0:keys] = wide[0 : 2 * keys, :].astype(BF).reshape(keys, 2, HEAD)
        dkv_store(g, slot).start()
        return carry

    lax.fori_loop(0, groups, backward, 0)
    settle(d_out, d_in, d_recv, d_send, 1, dq_ref)

    for n, result in enumerate((attended_ref, dq_ref)):
        leave_copy(n).wait_recv()
        for h in range(GROUP):
            cols = slice(h * HEAD, (h + 1) * HEAD)
            total = stay[n, :, cols] + arrived[n, :, cols].astype(F32)
            result[:, cols] = (gate * total if n == 0 else total).astype(BF)

    send_q.wait_send()
    send_g.wait_send()
    for n in range(7):
        hand_on(q_all, q_send, q_recv, 2, n).wait_send()
        hand_on(g_all, g_send, g_recv, 2, n).wait_send()
    for n in range(1, groups):
        stat_copy(0, n).wait_send()
        remote(fin_out.at[0], fin_in.at[0], fin_send.at[n], fin_recv.at[0], (row, other)).wait_send()
        part_copy(o_out, o_in, o_send, o_recv, 0, n - 1).wait_send()
        part_copy(d_out, d_in, d_send, d_recv, 0, n - 1).wait_send()
    up.wait_send()
    down.wait_send()
    for n in range(2):
        leave_copy(n).wait_send()
        dkv_store(0, n).wait()


def shards(queries, image_key_value, image_spans, tile_counts, cross_gate, grad_out):
    groups = lax.axis_size("enc")
    keys = image_key_value.shape[2]
    padded = chunks(keys, 256)[0]
    kv = image_key_value.reshape(2, keys, groups, HEAD).transpose(1, 2, 0, 3)
    wide = GROUP * HEAD
    vmem = pl.BlockSpec(memory_space=pltpu.VMEM)
    smem = pl.BlockSpec(memory_space=pltpu.SMEM)
    anywhere = pl.BlockSpec(memory_space=pl.ANY)
    block = pltpu.VMEM((SLOTS, wide), BF)
    pair = pltpu.VMEM((2, SLOTS, wide), BF)
    every = pltpu.VMEM((groups, SLOTS, wide), BF)
    stats = pltpu.VMEM((groups, 2, GROUP, SLOTS), F32)
    two_stats = pltpu.VMEM((2, 2, GROUP, SLOTS), F32)
    text = jax.ShapeDtypeStruct((SLOTS, wide), BF)
    sems = [2, 2, 2, 2, 7, 8, 7, 8, 8, 8, 2, 2, 8, 8, 7, 8, 7, 8, 2, 2]
    attended, grad_queries, dkv = pl.pallas_call(
        functools.partial(step_kernel, keys),
        out_shape=[text, text, jax.ShapeDtypeStruct(kv.shape, BF)],
        in_specs=[vmem, vmem, anywhere, smem, smem, smem],
        out_specs=[vmem, vmem, anywhere],
        scratch_shapes=[
            block,
            block,
            block,
            pair,
            pair,
            every,
            every,
            pltpu.VMEM((2, padded, 2, HEAD), BF),
            pltpu.VMEM((2, padded, 2, HEAD), BF),
            pltpu.VMEM((2 * padded, HEAD), F32),
            pltpu.VMEM((padded, HEAD), BF),
            pltpu.VMEM((padded, HEAD), BF),
            pltpu.VMEM((HEAD, padded), BF),
            pltpu.VMEM((padded, ROWS), F32),
            pltpu.VMEM((groups, padded, ROWS), BF),
            pltpu.VMEM((groups, HEAD, ROWS), F32),
            pltpu.VMEM((HEAD, ROWS), F32),
            pltpu.VMEM((groups, GROUP, SLOTS), F32),
            stats,
            stats,
            two_stats,
            two_stats,
            two_stats,
            stats,
            pltpu.VMEM((3, GROUP, SLOTS), F32),
            every,
            every,
            every,
            every,
            pltpu.VMEM((2, SLOTS, wide), F32),
            pair,
            pair,
        ]
        + [pltpu.SemaphoreType.DMA((n,)) for n in sems],
        compiler_params=pltpu.CompilerParams(
            collective_id=0, has_side_effects=True, vmem_limit_bytes=63 * 2**20
        ),
    )(queries, grad_out, kv, image_spans, tile_counts, cross_gate)
    grad_image_kv = dkv.transpose(2, 0, 1, 3).reshape(2, 1, keys, groups * HEAD)
    return attended, grad_queries, grad_image_kv


def solution(mesh):
    kv_part = P(None, ("seq", "enc"), None, None)
    return jax.shard_map(
        shards,
        mesh=mesh,
        in_specs=(P("seq", "enc"), kv_part, P(), P(), P(), P("seq", "enc")),
        out_specs=(P("seq", "enc"), P("seq", "enc"), kv_part),
        check_vma=False,
    )
```

time: 259 us -> 136 us (0.53)
  waiting for transfers between devices: 83.5 us -> 0 us
  blocking collectives: 53.7 us -> 0 us
  Pallas kernels: 69.8 us -> 122 us
  starting transfers between devices: 32.8 us -> 0 us
  other arithmetic: 5.1 us -> 0 us
    all_to_all x4 -> x0, waiting for transfers between devices: 56.1 us -> none  [exchange(): return lax.all_to_all(x, 'enc', split_axis=0, concat_axis=0, tiled=True)]
    all_to_all x1 -> x0, blocking collectives: 53.7 us -> none  [exchange(): return lax.all_to_all(x, 'enc', split_axis=0, concat_axis=0, tiled=True)]
    pallas_call x2 -> x1, Pallas kernels: 69.8 us -> 122 us  [shards(): pl.pallas_call(functools.partial(step_kernel, keys), out_shape=[text, tex...]
    ppermute x5 -> x0, waiting for transfers between devices: 27.4 us -> none  [shifted(): return lax.ppermute(x, 'seq', [(i, (i + by) % n) for i in range(n)])]
    all_to_all x4 -> x0, starting transfers between devices: 21 us -> none  [exchange(): return lax.all_to_all(x, 'enc', split_axis=0, concat_axis=0, tiled=True)]
    ppermute x5 -> x0, starting transfers between devices: 11.8 us -> none  [shifted(): return lax.ppermute(x, 'seq', [(i, (i + by) % n) for i in range(n)])]
    unnamed x6 -> x4, local copies, waits for them, and re-layouts: 0.02 us -> 11.6 us
    gather x10 -> x0, local copies, waits for them, and re-layouts: 6.54 us -> none  [the longest x6 3.95 us: slot_masks(): start, end = (spans[images, 0], spans[images, 1])]
  transfers between devices with their start and end apart: 9 -> 0, of which waited for: 8 -> 0; matrix products, arithmetic and copies ran while one was open for 3% -> 0% of each run, Pallas kernels for 0% -> 0%
where the time goes in v2:
time: 136 us; the launch traced here: 135 us
  Pallas kernels  122 us (90%)
  local copies, waits for them, and re-layouts  11.6 us (9%)
    pallas_call x1, Pallas kernels, shards(): pl.pallas_call(functools.partial(step_kernel, keys), out_shape=[text, tex...  122 us
    unnamed x4, local copies, waits for them, and re-layouts  11.6 us

profile of v2, /device:TPU:1, one launch (start us, length us, event | category | flops | bytes accessed | tf_op | source)
XLA Modules:
  0.0 134.9 jit_solution(6332916540650437209)
XLA Ops:
  1.3 1.4 %copy.9.spans = s32[32,2]{1,0:T(8,128)} copy(s32[32,2]{0,1:T(2,128)} %param.8) | data formatting | bytes 512 | tf_op args[2]
  2.6 122.0 %shard_map.85 = (bf16[128,1024]{1,0:T(8,128)(2,1)}, bf16[128,1024]{1,0:T(8,128)(2,1)}, bf16[1601,8,2,128]{3,2,1,0:T(2,128)(2,1)}) custom-call(bf16[128,1024]{1,0:T(8,128)(2,1)} %q_ref.1, bf16[128,1024]{1,0:T(8,128)(2,1)} %g_ref.1, bf16[1601,8,2,128]{3,2,1,0:T(2,128)(2,1)} %bitcast.6, s32[32,2]{1,0:T(8,128)} %copy.9.spans, s32[32]{0:T(128)} %counts.1, ...), custom_call_target="tpu_custom_call" | custom-call | tf_op jit(solution)/shard_map/pallas_call | solution.py:468
  124.7 1.7 %copy.14 = bf16[128,1024]{1,0:T(8,128)(2,1)} copy(bf16[128,1024]{1,0:T(8,128)(2,1)} %get-tuple-element.12) | data formatting | bytes 524288
  126.3 1.7 %copy.15 = bf16[128,1024]{1,0:T(8,128)(2,1)} copy(bf16[128,1024]{1,0:T(8,128)(2,1)} %get-tuple-element.13) | data formatting | bytes 524288
  128.0 6.9 %copy.16 = bf16[2,1,1601,1024]{3,0,2,1:T(2,128)(2,1)} copy(bf16[2,1,1601,1024]{3,0,2,1:T(2,128)(2,1)} %bitcast.7) | data formatting | bytes 13115392

commit v3 on v2

--- a/solution.py
+++ b/solution.py
@@ -78,6 +78,7 @@
 
 
 MESH = pl.DeviceIdType.MESH
+LAG = 3
 
 
 def merged(entries):
@@ -97,8 +98,8 @@
 
 def step_kernel(
     keys,
-    q_ref,
-    g_ref,
+    q_hbm,
+    g_hbm,
     kv_ref,
     spans,
     counts,
@@ -106,6 +107,8 @@
     attended_ref,
     dq_ref,
     dkv_ref,
+    q_ref,
+    g_ref,
     g_low,
     next_q,
     next_g,
@@ -132,12 +135,15 @@
     fin_in,
     weight,
     o_out,
+    o_sib,
     o_in,
     d_out,
+    d_sib,
     d_in,
     stay,
     leave,
     arrived,
+    text_sem,
     kv_sem,
     dkv_sem,
     next_send,
@@ -152,8 +158,12 @@
     seq_recv,
     fin_send,
     fin_recv,
+    o_sib_send,
+    o_sib_recv,
     o_send,
     o_recv,
+    d_sib_send,
+    d_sib_recv,
     d_send,
     d_recv,
     leave_send,
@@ -185,6 +195,12 @@
     def dkv_store(g, slot):
         return pltpu.make_async_copy(dkv_buf.at[slot, 0:keys], dkv_ref.at[:, g], dkv_sem.at[slot])
 
+    text = [
+        pltpu.make_async_copy(q_hbm, q_ref, text_sem.at[0]),
+        pltpu.make_async_copy(g_hbm, g_ref, text_sem.at[1]),
+    ]
+    for copy in text:
+        copy.start()
     kv_load(group_at(0), 0).start()
 
     barrier = pltpu.get_barrier_semaphore()
@@ -195,8 +211,10 @@
     pl.semaphore_wait(barrier, groups + 1)
 
     to_below = (below, me)
+    text[0].wait()
     send_q = remote(q_ref, next_q, next_send.at[0], next_recv.at[0], to_below)
     send_q.start()
+    text[1].wait()
     gate = jnp.tanh(jnp.full((SLOTS, HEAD), gate_ref[0], F32))
     for h in range(GROUP):
         cols = slice(h * HEAD, (h + 1) * HEAD)
@@ -204,8 +222,8 @@
     send_g = remote(g_low, next_g, next_send.at[1], next_recv.at[1], to_below)
     send_g.start()
 
-    starts = [spans[2 * row + i, 0] for i in range(2)]
-    ends = [spans[2 * row + i, 1] for i in range(2)]
+    starts = [spans[0, 2 * row + i] for i in range(2)]
+    ends = [spans[1, 2 * row + i] for i in range(2)]
     used = [counts[2 * row + i] for i in range(2)]
     at_rows = row * SLOTS + lax.broadcasted_iota(jnp.int32, (SLOTS, HEAD), 0)
     at_lanes = row * SLOTS + lax.broadcasted_iota(jnp.int32, (GROUP, SLOTS), 1)
@@ -235,8 +253,15 @@
 
     send_q.wait_recv()
     fan_out(q_ref, next_q, pick_q, q_all, q_send, q_recv)
-    send_g.wait_recv()
-    fan_out(g_low, next_g, pick_g, g_all, g_send, g_recv)
+
+    def stat_copy(g, n):
+        return remote(stat_out.at[g], stat_in.at[me], stat_send.at[n], stat_recv.at[me], (row, g))
+
+    def delta(g):
+        for h in range(GROUP):
+            lanes = slice(h * SLOTS, (h + 1) * SLOTS)
+            g_t = g_all[g, :, h * HEAD : (h + 1) * HEAD].T.astype(F32)
+            stat_out[g, 1, h : h + 1, :] = jnp.sum(out_t[g, :, lanes] * g_t, axis=0, keepdims=True)
 
     def forward(i, carry):
         g = group_at(i)
@@ -248,7 +273,13 @@
         def _():
             arrival(q_all, q_send, q_recv, g).wait_recv()
 
+        @pl.when(i == 1)
+        def _():
+            send_g.wait_recv()
+            fan_out(g_low, next_g, pick_g, g_all, g_send, g_recv)
+
         for n in range(3):
+
             @pl.when(i == 2 + 2 * n)
             def _():
                 hand_on(q_all, q_send, q_recv, 2 + 2 * n, 4 + n).start()
@@ -257,6 +288,18 @@
             def _():
                 arrival(g_all, g_send, g_recv, group_at(2 + 2 * n)).wait_recv()
                 hand_on(g_all, g_send, g_recv, 2 + 2 * n, 4 + n).start()
+
+        late = group_at(jnp.maximum(i - LAG, 0))
+
+        @pl.when((i > LAG) & ((i - LAG) % 2 == 1))
+        def _():
+            arrival(g_all, g_send, g_recv, late).wait_recv()
+
+        delta(late)
+
+        @pl.when(i > LAG)
+        def _():
+            stat_copy(late, i - LAG).start()
 
         split_tile(keys, kv_buf[slot, 0:keys], wide, k_pad, v_pad)
         turned[...] = v_pad[...].T
@@ -271,28 +314,12 @@
 
     lax.fori_loop(0, groups, forward, 0)
 
-    def stat_copy(g, n):
-        return remote(stat_out.at[g], stat_in.at[me], stat_send.at[n], stat_recv.at[me], (row, g))
-
-    def delta(i, carry):
-        g = group_at(i)
-
-        @pl.when(i % 2 == 1)
-        def _():
-            arrival(g_all, g_send, g_recv, g).wait_recv()
-
-        for h in range(GROUP):
-            lanes = slice(h * SLOTS, (h + 1) * SLOTS)
-            g_t = g_all[g, :, h * HEAD : (h + 1) * HEAD].T.astype(F32)
-            stat_out[g, 1, h : h + 1, :] = jnp.sum(out_t[g, :, lanes] * g_t, axis=0, keepdims=True)
-
-        @pl.when(i > 0)
-        def _():
-            stat_copy(g, i).start()
-
-        return carry
-
-    lax.fori_loop(0, groups, delta, 0)
+    for i in range(TILES * 2 - LAG, TILES * 2):
+        late = group_at(i)
+        if i % 2 == 1:
+            arrival(g_all, g_send, g_recv, late).wait_recv()
+        delta(late)
+        stat_copy(late, i).start()
     stat_in[me] = stat_out[me]
     for j in range(1, groups):
         src = (me + j) % groups
@@ -329,28 +356,48 @@
         remote(fin_out.at[c // TILES], fin_in.at[me], fin_send.at[j], fin_recv.at[me], (row, c)).start()
 
     my_used = counts[2 * row + image]
-    my_start = spans[2 * row + image, 0]
-    my_end = jnp.where(me % TILES < my_used, spans[2 * row + image, 1], 0)
+    my_start = spans[0, 2 * row + image]
+    my_end = jnp.where(me % TILES < my_used, spans[1, 2 * row + image], 0)
     shown = ((at_lanes >= my_start) & (at_lanes < my_end)) | (
         (at_lanes + SLOTS >= my_start) & (at_lanes + SLOTS < my_end)
     )
 
-    def part_copy(out, dest, send, recv, g, n):
-        return remote(out.at[g], dest.at[me], send.at[n], recv.at[me], (row, g))
-
-    def settle(out, dest, recv, send, n, result):
-        for j in range(1, groups):
-            src = (me + j) % groups
-            remote(out.at[0], dest.at[src], send.at[0], recv.at[src], (row, src)).wait_recv()
-        dest[me] = out[me]
+    def to_sibling(out, sib, send, recv, g, j):
+        return remote(out.at[g], sib.at[j], send.at[j], recv.at[j], (row, other))
+
+    def to_owner(out, dest, send, recv, g, j):
+        return remote(out.at[g], dest.at[z], send.at[j], recv.at[z], (row, g))
+
+    def pass_on(values, out, sib, dest, sib_send, sib_recv, send, recv, i, g):
+        j = (groups - 1 - i) // 2
+
+        @pl.when(i % 2 == 0)
+        def _():
+            for h in range(GROUP):
+                out[g, :, h * HEAD : (h + 1) * HEAD] = values(h).astype(BF)
+            to_sibling(out, sib, sib_send, sib_recv, g, j).start()
+
+        @pl.when(i % 2 == 1)
+        def _():
+            to_sibling(out, sib, sib_send, sib_recv, g, j).wait_recv()
+            for h in range(GROUP):
+                cols = slice(h * HEAD, (h + 1) * HEAD)
+                out[g, :, cols] = (values(h) + sib[j, :, cols].astype(F32)).astype(BF)
+
+        @pl.when((i % 2 == 1) & (i < groups - 1))
+        def _():
+            to_owner(out, dest, send, recv, g, j).start()
+
+    def settle(out, dest, recv, send, n):
+        for j in range(1, chips):
+            src = (z + j) % chips
+            remote(out.at[0], dest.at[src], send.at[0], recv.at[src], (row, 2 * src + core)).wait_recv()
+        dest[z] = out[me]
         for h in range(GROUP):
             cols = slice(h * HEAD, (h + 1) * HEAD)
             sums = []
             for i in range(2):
-                total = dest[TILES * i, :, cols].astype(F32)
-                for c in range(1, TILES):
-                    total = total + dest[TILES * i + c, :, cols].astype(F32)
-                sums.append(total)
+                sums.append(dest[2 * i, :, cols].astype(F32) + dest[2 * i + 1, :, cols].astype(F32))
             kept = [jnp.where(own_rows[i], sums[i], 0.0) for i in range(2)]
             gone = [jnp.where(own_rows[i], 0.0, sums[i]) for i in range(2)]
             stay[n, :, cols] = kept[0] + kept[1]
@@ -378,18 +425,14 @@
         def lanes_of(n):
             return jnp.concatenate([weight[n, h : h + 1, :] for h in range(GROUP)], 1)
 
-        for h in range(GROUP):
-            lanes = slice(h * SLOTS, (h + 1) * SLOTS)
-            cols = slice(h * HEAD, (h + 1) * HEAD)
-            o_out[g, :, cols] = (out_t[g, :, lanes] * weight[1, h : h + 1, :]).T.astype(BF)
-
-        @pl.when(i < groups - 1)
-        def _():
-            part_copy(o_out, o_in, o_send, o_recv, g, i).start()
+        def o_rows(h):
+            return (out_t[g, :, h * SLOTS : (h + 1) * SLOTS] * weight[1, h : h + 1, :]).T
+
+        pass_on(o_rows, o_out, o_sib, o_in, o_sib_send, o_sib_recv, o_send, o_recv, i, g)
 
         @pl.when(i == groups - 1)
         def _():
-            settle(o_out, o_in, o_recv, o_send, 0, attended_ref)
+            settle(o_out, o_in, o_recv, o_send, 0)
 
         @pl.when(i >= 2)
         def _():
@@ -409,21 +452,16 @@
             dq_t,
             wide,
         )
-        for h in range(GROUP):
-            lanes = slice(h * SLOTS, (h + 1) * SLOTS)
-            cols = slice(h * HEAD, (h + 1) * HEAD)
-            d_out[g, :, cols] = (dq_t[:, lanes] * SCALE).T.astype(BF)
-
-        @pl.when(i < groups - 1)
-        def _():
-            part_copy(d_out, d_in, d_send, d_recv, g, i).start()
-
+        def d_rows(h):
+            return (dq_t[:, h * SLOTS : (h + 1) * SLOTS] * SCALE).T
+
+        pass_on(d_rows, d_out, d_sib, d_in, d_sib_send, d_sib_recv, d_send, d_recv, i, g)
         dkv_buf[slot, 0:keys] = wide[0 : 2 * keys, :].astype(BF).reshape(keys, 2, HEAD)
         dkv_store(g, slot).start()
         return carry
 
     lax.fori_loop(0, groups, backward, 0)
-    settle(d_out, d_in, d_recv, d_send, 1, dq_ref)
+    settle(d_out, d_in, d_recv, d_send, 1)
 
     for n, result in enumerate((attended_ref, dq_ref)):
         leave_copy(n).wait_recv()
@@ -440,13 +478,34 @@
     for n in range(1, groups):
         stat_copy(0, n).wait_send()
         remote(fin_out.at[0], fin_in.at[0], fin_send.at[n], fin_recv.at[0], (row, other)).wait_send()
-        part_copy(o_out, o_in, o_send, o_recv, 0, n - 1).wait_send()
-        part_copy(d_out, d_in, d_send, d_recv, 0, n - 1).wait_send()
+    for j in range(chips):
+        to_sibling(o_out, o_sib, o_sib_send, o_sib_recv, 0, j).wait_send()
+        to_sibling(d_out, d_sib, d_sib_send, d_sib_recv, 0, j).wait_send()
+    for j in range(1, chips):
+        remote(o_out.at[0], o_in.at[0], o_send.at[j], o_recv.at[0], (row, other)).wait_send()
+        remote(d_out.at[0], d_in.at[0], d_send.at[j], d_recv.at[0], (row, other)).wait_send()
     up.wait_send()
     down.wait_send()
     for n in range(2):
         leave_copy(n).wait_send()
         dkv_store(0, n).wait()
+
+
+def finish_kernel(pieces, a_in, d_in, kv_in, a_out, d_out, kv_out, a_buf, d_buf, kv_buf, loads, stores):
+    keys = kv_in.shape[0]
+    step = -(-keys // pieces)
+    parts = [slice(n * step, min((n + 1) * step, keys)) for n in range(pieces)]
+    moves = [(a_in, a_buf, a_out), (d_in, d_buf, d_out)]
+    moves += [(kv_in.at[p], kv_buf.at[p], kv_out.at[p]) for p in parts]
+    into = [pltpu.make_async_copy(m[0], m[1], loads.at[n]) for n, m in enumerate(moves)]
+    out = [pltpu.make_async_copy(m[1], m[2], stores.at[n]) for n, m in enumerate(moves)]
+    for copy in into:
+        copy.start()
+    for copy, store in zip(into, out):
+        copy.wait()
+        store.start()
+    for store in out:
+        store.wait()
 
 
 def shards(queries, image_key_value, image_spans, tile_counts, cross_gate, grad_out):
@@ -461,16 +520,19 @@
     block = pltpu.VMEM((SLOTS, wide), BF)
     pair = pltpu.VMEM((2, SLOTS, wide), BF)
     every = pltpu.VMEM((groups, SLOTS, wide), BF)
+    quarter = pltpu.VMEM((groups // 2, SLOTS, wide), BF)
     stats = pltpu.VMEM((groups, 2, GROUP, SLOTS), F32)
     two_stats = pltpu.VMEM((2, 2, GROUP, SLOTS), F32)
     text = jax.ShapeDtypeStruct((SLOTS, wide), BF)
-    sems = [2, 2, 2, 2, 7, 8, 7, 8, 8, 8, 2, 2, 8, 8, 7, 8, 7, 8, 2, 2]
+    sems = [2, 2, 2, 2, 2, 7, 8, 7, 8, 8, 8, 2, 2, 8, 8] + [4] * 8 + [2, 2]
     attended, grad_queries, dkv = pl.pallas_call(
         functools.partial(step_kernel, keys),
         out_shape=[text, text, jax.ShapeDtypeStruct(kv.shape, BF)],
-        in_specs=[vmem, vmem, anywhere, smem, smem, smem],
+        in_specs=[anywhere, anywhere, anywhere, smem, smem, smem],
         out_specs=[vmem, vmem, anywhere],
         scratch_shapes=[
+            block,
+            block,
             block,
             block,
             block,
@@ -497,9 +559,11 @@
             stats,
             pltpu.VMEM((3, GROUP, SLOTS), F32),
             every,
+            quarter,
+            quarter,
             every,
-            every,
-            every,
+            quarter,
+            quarter,
             pltpu.VMEM((2, SLOTS, wide), F32),
             pair,
             pair,
@@ -508,7 +572,17 @@
         compiler_params=pltpu.CompilerParams(
             collective_id=0, has_side_effects=True, vmem_limit_bytes=63 * 2**20
         ),
-    )(queries, grad_out, kv, image_spans, tile_counts, cross_gate)
+    )(queries, grad_out, kv, image_spans.T, tile_counts, cross_gate)
+    pieces = 16
+    attended, grad_queries, dkv = pl.pallas_call(
+        functools.partial(finish_kernel, pieces),
+        out_shape=[text, text, jax.ShapeDtypeStruct(kv.shape, BF)],
+        in_specs=[anywhere] * 3,
+        out_specs=[anywhere] * 3,
+        scratch_shapes=[block, block, pltpu.VMEM(kv.shape, BF)]
+        + [pltpu.SemaphoreType.DMA((pieces + 2,))] * 2,
+        compiler_params=pltpu.CompilerParams(vmem_limit_bytes=62 * 2**20),
+    )(attended, grad_queries, dkv)
     grad_image_kv = dkv.transpose(2, 0, 1, 3).reshape(2, 1, keys, groups * HEAD)
     return attended, grad_queries, grad_image_kv
 

time: 136 us -> 118 us (0.87)
  local copies, waits for them, and re-layouts: 11.6 us -> 0 us
  Pallas kernels: 122 us -> 117 us
    unnamed x4 -> x0, local copies, waits for them, and re-layouts: 11.6 us -> none
    pallas_call x1, Pallas kernels: 122 us -> 111 us  [shards(): pl.pallas_call(functools.partial(step_kernel, keys), out_shape=[text, tex...]
    pallas_call x0 -> x1, Pallas kernels: none -> 5.74 us  [shards(): pl.pallas_call(functools.partial(finish_kernel, pieces), out_shape=[text,...]
where the time goes in v3:
time: 118 us
  Pallas kernels  117 us (99%)
  between operations  1.29 us (1%)
    pallas_call x1, Pallas kernels, shards(): pl.pallas_call(functools.partial(step_kernel, keys), out_shape=[text, tex...  111 us
    pallas_call x1, Pallas kernels, shards(): pl.pallas_call(functools.partial(finish_kernel, pieces), out_shape=[text,...  5.74 us

profile of v3, /device:TPU:1, one launch (start us, length us, event | category | flops | bytes accessed | tf_op | source)
XLA Modules:
  0.0 118.0 jit_solution(15530217286113293907)
XLA Ops:
  1.3 111.0 %shard_map.85 = (bf16[128,1024]{1,0:T(8,128)(2,1)}, bf16[128,1024]{1,0:T(8,128)(2,1)}, bf16[1601,8,2,128]{3,2,1,0:T(2,128)(2,1)}) custom-call(bf16[128,1024]{1,0:T(8,128)(2,1)} %q_hbm.1, bf16[128,1024]{1,0:T(8,128)(2,1)} %g_hbm.1, bf16[1601,8,2,128]{3,2,1,0:T(2,128)(2,1)} %bitcast.7, s32[2,32]{1,0:T(2,128)} %bitcast.8, s32[32]{0:T(128)} %counts.1, ...), custom_call_target="tpu_custom_call" | custom-call | tf_op jit(solution)/shard_map/pallas_call | solution.py:528
  112.2 5.7 %shard_map.86 = (bf16[128,1024]{1,0:T(8,128)(2,1)}, bf16[128,1024]{1,0:T(8,128)(2,1)}, bf16[1601,8,2,128]{3,2,1,0:T(2,128)(2,1)}) custom-call(bf16[128,1024]{1,0:T(8,128)(2,1)} %get-tuple-element.9.a_in, bf16[128,1024]{1,0:T(8,128)(2,1)} %get-tuple-element.10.d_in, bf16[1601,8,2,128]{3,2,1,0:T(2,128)(2,1)} %get-tuple-element.11.kv_in), custom_call_target="tpu_custom_call" | custom-call | tf_op jit(solution)/shard_map/pallas_call | solution.py:577

commit v4 on v3

--- a/solution.py
+++ b/solution.py
@@ -43,7 +43,7 @@
 
 
 def forward_group(keys, k_pad, v_t, q, probs, scores, out_t):
-    padded, parts = chunks(keys, 256)
+    padded, parts = chunks(keys, 896)
     top = jnp.full((8, ROWS), NEG, F32)
     for o, n in parts:
         s = dot(k_pad[o : o + n, :], q, NT)
@@ -66,7 +66,7 @@
 
 
 def backward_group(keys, v_pad, k_t, q, g, probs, factor, delta, dq_t, wide):
-    padded, parts = chunks(keys, 256)
+    padded, parts = chunks(keys, 896)
     for o, n in parts:
         dp = dot(v_pad[o : o + n, :], g, NT)
         p = probs[o : o + n, :].astype(F32) * factor
@@ -79,6 +79,7 @@
 
 MESH = pl.DeviceIdType.MESH
 LAG = 3
+PIECE = 2
 
 
 def merged(entries):
@@ -402,10 +403,15 @@
             gone = [jnp.where(own_rows[i], 0.0, sums[i]) for i in range(2)]
             stay[n, :, cols] = kept[0] + kept[1]
             leave[n, :, cols] = (gone[0] + gone[1]).astype(BF)
-        leave_copy(n).start()
-
-    def leave_copy(n):
-        return remote(leave.at[n], arrived.at[n], leave_send.at[n], leave_recv.at[n], (above, me))
+            if h % PIECE == PIECE - 1:
+                leave_copy(n, h // PIECE).start()
+
+    def leave_copy(n, k):
+        cols = slice(k * PIECE * HEAD, (k + 1) * PIECE * HEAD)
+        sem = n * (GROUP // PIECE) + k
+        return remote(
+            leave.at[n, :, cols], arrived.at[n, :, cols], leave_send.at[sem], leave_recv.at[sem], (above, me)
+        )
 
     def backward(i, carry):
         g = group_at(groups - 1 - i)
@@ -464,8 +470,9 @@
     settle(d_out, d_in, d_recv, d_send, 1)
 
     for n, result in enumerate((attended_ref, dq_ref)):
-        leave_copy(n).wait_recv()
         for h in range(GROUP):
+            if h % PIECE == 0:
+                leave_copy(n, h // PIECE).wait_recv()
             cols = slice(h * HEAD, (h + 1) * HEAD)
             total = stay[n, :, cols] + arrived[n, :, cols].astype(F32)
             result[:, cols] = (gate * total if n == 0 else total).astype(BF)
@@ -487,7 +494,8 @@
     up.wait_send()
     down.wait_send()
     for n in range(2):
-        leave_copy(n).wait_send()
+        for k in range(GROUP // PIECE):
+            leave_copy(n, k).wait_send()
         dkv_store(0, n).wait()
 
 
@@ -511,7 +519,7 @@
 def shards(queries, image_key_value, image_spans, tile_counts, cross_gate, grad_out):
     groups = lax.axis_size("enc")
     keys = image_key_value.shape[2]
-    padded = chunks(keys, 256)[0]
+    padded = chunks(keys, 896)[0]
     kv = image_key_value.reshape(2, keys, groups, HEAD).transpose(1, 2, 0, 3)
     wide = GROUP * HEAD
     vmem = pl.BlockSpec(memory_space=pltpu.VMEM)
@@ -524,7 +532,7 @@
     stats = pltpu.VMEM((groups, 2, GROUP, SLOTS), F32)
     two_stats = pltpu.VMEM((2, 2, GROUP, SLOTS), F32)
     text = jax.ShapeDtypeStruct((SLOTS, wide), BF)
-    sems = [2, 2, 2, 2, 2, 7, 8, 7, 8, 8, 8, 2, 2, 8, 8] + [4] * 8 + [2, 2]
+    sems = [2, 2, 2, 2, 2, 7, 8, 7, 8, 8, 8, 2, 2, 8, 8] + [4] * 8 + [8, 8]
     attended, grad_queries, dkv = pl.pallas_call(
         functools.partial(step_kernel, keys),
         out_shape=[text, text, jax.ShapeDtypeStruct(kv.shape, BF)],

time: 118 us -> 119 us (level)
  no operation moved by 1% of the time
where the time goes in v4:
time: 119 us
  Pallas kernels  117 us (98%)
  between operations  1.29 us (1%)
    pallas_call x1, Pallas kernels, shards(): pl.pallas_call(functools.partial(step_kernel, keys), out_shape=[text, tex...  112 us
    pallas_call x1, Pallas kernels, shards(): pl.pallas_call(functools.partial(finish_kernel, pieces), out_shape=[text,...  5.74 us

profile of v4, /device:TPU:1, one launch (start us, length us, event | category | flops | bytes accessed | tf_op | source)
XLA Modules:
  0.0 118.7 jit_solution(8068186508973993019)
XLA Ops:
  1.3 111.7 %shard_map.85 = (bf16[128,1024]{1,0:T(8,128)(2,1)}, bf16[128,1024]{1,0:T(8,128)(2,1)}, bf16[1601,8,2,128]{3,2,1,0:T(2,128)(2,1)}) custom-call(bf16[128,1024]{1,0:T(8,128)(2,1)} %q_hbm.1, bf16[128,1024]{1,0:T(8,128)(2,1)} %g_hbm.1, bf16[1601,8,2,128]{3,2,1,0:T(2,128)(2,1)} %bitcast.7, s32[2,32]{1,0:T(2,128)} %bitcast.8, s32[32]{0:T(128)} %counts.1, ...), custom_call_target="tpu_custom_call" | custom-call | tf_op jit(solution)/shard_map/pallas_call | solution.py:536
  113.0 5.7 %shard_map.86 = (bf16[128,1024]{1,0:T(8,128)(2,1)}, bf16[128,1024]{1,0:T(8,128)(2,1)}, bf16[1601,8,2,128]{3,2,1,0:T(2,128)(2,1)}) custom-call(bf16[128,1024]{1,0:T(8,128)(2,1)} %get-tuple-element.9.a_in, bf16[128,1024]{1,0:T(8,128)(2,1)} %get-tuple-element.10.d_in, bf16[1601,8,2,128]{3,2,1,0:T(2,128)(2,1)} %get-tuple-element.11.kv_in), custom_call_target="tpu_custom_call" | custom-call | tf_op jit(solution)/shard_map/pallas_call | solution.py:585

commit v5 on v3

--- a/solution.py
+++ b/solution.py
@@ -412,6 +412,9 @@
         slot = i % 2
         kv_load(g, slot).wait()
 
+        split_tile(keys, kv_buf[slot, 0:keys], wide, k_pad, v_pad)
+        turned[...] = k_pad[...].T
+
         @pl.when(i < groups - 1)
         def _():
             kv_load(group_at(groups - 2 - i), 1 - slot).start()
@@ -438,8 +441,6 @@
         def _():
             dkv_store(g, slot).wait()
 
-        split_tile(keys, kv_buf[slot, 0:keys], wide, k_pad, v_pad)
-        turned[...] = k_pad[...].T
         backward_group(
             keys,
             v_pad,

time: 118 us -> 120 us (1.017)
  Pallas kernels: 117 us -> 119 us
    pallas_call x1, Pallas kernels: 111 us -> 113 us  [shards(): pl.pallas_call(functools.partial(step_kernel, keys), out_shape=[text, tex...]
where the time goes in v5:
time: 120 us
  Pallas kernels  119 us (99%)
  between operations  1.29 us (1%)
    pallas_call x1, Pallas kernels, shards(): pl.pallas_call(functools.partial(step_kernel, keys), out_shape=[text, tex...  113 us
    pallas_call x1, Pallas kernels, shards(): pl.pallas_call(functools.partial(finish_kernel, pieces), out_shape=[text,...  5.74 us

profile of v5, /device:TPU:1, one launch (start us, length us, event | category | flops | bytes accessed | tf_op | source)
XLA Modules:
  0.0 119.9 jit_solution(12125285112160240324)
XLA Ops:
  1.3 112.9 %shard_map.85 = (bf16[128,1024]{1,0:T(8,128)(2,1)}, bf16[128,1024]{1,0:T(8,128)(2,1)}, bf16[1601,8,2,128]{3,2,1,0:T(2,128)(2,1)}) custom-call(bf16[128,1024]{1,0:T(8,128)(2,1)} %q_hbm.1, bf16[128,1024]{1,0:T(8,128)(2,1)} %g_hbm.1, bf16[1601,8,2,128]{3,2,1,0:T(2,128)(2,1)} %bitcast.7, s32[2,32]{1,0:T(2,128)} %bitcast.8, s32[32]{0:T(128)} %counts.1, ...), custom_call_target="tpu_custom_call" | custom-call | tf_op jit(solution)/shard_map/pallas_call | solution.py:529
  114.2 5.7 %shard_map.86 = (bf16[128,1024]{1,0:T(8,128)(2,1)}, bf16[128,1024]{1,0:T(8,128)(2,1)}, bf16[1601,8,2,128]{3,2,1,0:T(2,128)(2,1)}) custom-call(bf16[128,1024]{1,0:T(8,128)(2,1)} %get-tuple-element.9.a_in, bf16[128,1024]{1,0:T(8,128)(2,1)} %get-tuple-element.10.d_in, bf16[1601,8,2,128]{3,2,1,0:T(2,128)(2,1)} %get-tuple-element.11.kv_in), custom_call_target="tpu_custom_call" | custom-call | tf_op jit(solution)/shard_map/pallas_call | solution.py:578
